TPU v7x, 32 devices: a whole 2x2x4 slice. The times are simulated.
32 devices in a mesh: dp: 16 (over z, x, core), mp: 2 (over y).
Axes of the slice: x: 2, y: 2, z: 4, core: 2. Of those that a mesh axis runs over, the one named last changes fastest.
Arguments:
- residual: bfloat16 [4096, 16, 768], P('mp', 'dp'), may hold values from -6 to 6
- out_grad: bfloat16 [4096, 16, 768], P('mp', 'dp'), may hold values from -6 to 6
- doc_bounds: int32 [16, 7], P('dp'), may hold values from 0 to 4096, as said below
- norm_gain: float32 [768], replicated, may hold values from 0.5 to 1.5
- proj_gate: bfloat16 [768, 1536], P(None, 'mp'), may hold values from -0.21875 to 0.21875
- proj_value: bfloat16 [768, 1536], P(None, 'mp'), may hold values from -0.21875 to 0.21875
- proj_state: bfloat16 [768, 256], replicated, may hold values from -0.21875 to 0.21875
- proj_step: bfloat16 [768, 48], P(None, 'mp'), may hold values from -0.21875 to 0.21875
- conv_value: float32 [4, 1536], P(None, 'mp'), may hold values from -3 to 3
- conv_value_bias: float32 [1536], P('mp'), may hold values from -3 to 3
- conv_state: float32 [4, 256], replicated, may hold values from -3 to 3
- conv_state_bias: float32 [256], replicated, may hold values from -3 to 3
- step_bias: float32 [48], P('mp'), may hold values from -6.9 to -2.3
- rate_log: float32 [24], P('mp'), may hold values from 0 to 2.77
- skip_gain: float32 [24], P('mp'), may hold values from 0.5 to 1.5
- skip_proj: bfloat16 [1536, 24], P('mp'), may hold values from -0.15625 to 0.15625
- mixer_gain: float32 [1536], P('mp'), may hold values from 0.5 to 1.5
- proj_out: bfloat16 [1536, 768], P('mp'), may hold values from -0.15625 to 0.15625
Outputs:
- output: bfloat16 [4096, 16, 768], P('mp', 'dp')
- grad_residual: float32 [4096, 16, 768], P('mp', 'dp')
- grad_norm_gain: float32 [768], replicated
- grad_proj_gate: float32 [768, 1536], P(None, 'mp')
- grad_proj_value: float32 [768, 1536], P(None, 'mp')
- grad_proj_state: float32 [768, 256], replicated
- grad_proj_step: float32 [768, 48], P(None, 'mp')
- grad_conv_value: float32 [4, 1536], P(None, 'mp')
- grad_conv_value_bias: float32 [1536], P('mp')
- grad_conv_state: float32 [4, 256], replicated
- grad_conv_state_bias: float32 [256], replicated
- grad_step_bias: float32 [48], P('mp')
- grad_rate_log: float32 [24], P('mp')
- grad_skip_gain: float32 [24], P('mp')
- grad_skip_proj: float32 [1536, 24], P('mp')
- grad_mixer_gain: float32 [1536], P('mp')
- grad_proj_out: float32 [1536, 768], P('mp')
Inputs may be any that keep to these rules, and one draw needn't show every extreme that they name: `doc_bounds`: in each row the entries never fall: entry 0 is 0, entry k below 6 is where document k starts, and entry 6 is where the padding starts, at least 2049.
All inputs are finite; a program needn't handle non-finite values.
Results may differ from a plain program's by a relative error of at most 0.02.
Values may be sent and summed in bfloat16 or wider, within the bound.
No kernel may reach another device: no remote copies, remote signals or barrier semaphores. Data moves between devices by JAX's collectives and lax.ppermute only.
A program may use at most 640 MiB of HBM per device.

v0:
```python
import math

import jax
import jax.numpy as jnp
from jax import lax
from jax.sharding import PartitionSpec as P

epsilon = 1e-05
highest = lax.Precision.HIGHEST


def as_operand(values):
    return values.astype(jnp.bfloat16)


def contract(form, left_op, right_op):
    return jnp.einsum(form, left_op, right_op, preferred_element_type=jnp.float32)


def segment_sums(values):
    count_all = values.shape[-1]
    places = jnp.arange(count_all)
    repeated = jnp.broadcast_to(values[..., :, None], values.shape + (count_all,))
    lower_mask = places[:, None] > places[None, :]
    running = jnp.cumsum(jnp.where(lower_mask, repeated, 0.0), axis=-2)
    return jnp.where(places[:, None] >= places[None, :], running, -jnp.inf)


def scan_direction(inputs, step_size, decays, keys_in, read_out, segment):
    length, head_count, head_width = inputs.shape
    state_width = keys_in.shape[1]
    block_len = math.gcd(length, 128)
    blocks = length // block_len
    weighted = (inputs * step_size[:, :, None]).reshape(blocks, block_len, head_count, head_width)
    log_decay = jnp.transpose(decays.reshape(blocks, block_len, head_count), (0, 2, 1))
    key_block = keys_in.reshape(blocks, block_len, state_width)
    read_block = read_out.reshape(blocks, block_len, state_width)
    seg_block = segment.reshape(blocks, block_len)
    places = jnp.arange(block_len)
    strict = (places[:, None] > places[None, :])[None] & (
        seg_block[:, :, None] == seg_block[:, None, :]
    )
    scores = contract("cin,cjn->cij", as_operand(read_block), as_operand(key_block))
    mixing = jnp.where(strict[:, None], jnp.exp(segment_sums(log_decay)), 0.0) * scores[:, None]
    inner_part = contract("chij,cjhp->cihp", as_operand(mixing), as_operand(weighted))
    running = jnp.cumsum(log_decay, axis=-1)
    to_end = jnp.exp(running[..., -1:] - running) * (seg_block == seg_block[:, -1:])[:, None, :]
    states = jnp.einsum("chj,cjn,cjhp->chpn", to_end, key_block, weighted, precision=highest)
    block_logs = jnp.transpose(running[..., -1])
    end_seg = seg_block[:, -1]
    carry_mix = jnp.exp(segment_sums(block_logs)) * (end_seg[:, None] == end_seg[None, :])[None]
    totals = jnp.einsum("hcd,dhpn->chpn", carry_mix, states, precision=highest)
    entering = jnp.concatenate([jnp.zeros_like(totals[:1]), totals[:-1]], 0)
    before = jnp.concatenate([seg_block[:1, :1], seg_block[:-1, -1:]], 0)
    reaching = jnp.exp(running) * (seg_block == before)[:, None, :]
    outer_part = jnp.einsum("cin,chpn,chi->cihp", read_block, entering, reaching, precision=highest)
    return (inner_part + outer_part).reshape(length, head_count, head_width)


def quasiseparable(mixed_in, gates_in, step_pre, step_bias, rate_log, segment):
    length, head_count, head_width = mixed_in.shape
    state_width = gates_in.shape[1] // 4
    step_size = jax.nn.softplus(
        step_pre.reshape(length, head_count, 2) + step_bias.reshape(head_count, 2)
    )
    decays = -step_size * jnp.exp(rate_log)[:, None]
    forward_part = scan_direction(
        mixed_in,
        step_size[:, :, 0],
        decays[:, :, 0],
        gates_in[:, :state_width],
        gates_in[:, state_width : 2 * state_width],
        segment,
    )
    backward_part = scan_direction(
        mixed_in[::-1],
        step_size[::-1, :, 1],
        decays[::-1, :, 1],
        gates_in[::-1, 2 * state_width : 3 * state_width],
        gates_in[::-1, 3 * state_width :],
        segment[::-1],
    )
    return forward_part + backward_part[::-1]


def short_conv(signal, kernel, offset, segment):
    length = signal.shape[0]
    result = offset + kernel[0] * signal
    for shift_by in range(1, kernel.shape[0]):
        delayed = jnp.concatenate(
            [jnp.zeros((shift_by, signal.shape[1]), signal.dtype), signal[: length - shift_by]], 0
        )
        delayed_seg = jnp.concatenate(
            [jnp.full((shift_by,), -1, segment.dtype), segment[: length - shift_by]], 0
        )
        result = result + kernel[shift_by] * delayed * (delayed_seg == segment)[:, None]
    return result


def conv_silu(value_in, state_in, kernel_v, offset_v, kernel_s, offset_s, segment):
    return (
        jax.nn.silu(short_conv(value_in, kernel_v, offset_v, segment)),
        jax.nn.silu(short_conv(state_in, kernel_s, offset_s, segment)),
    )


def segments_of(doc_bounds, length):
    places = jnp.arange(length, dtype=jnp.int32)
    segment = jnp.sum((places[None, :, None] >= doc_bounds[:, None, :]).astype(jnp.int32), -1)
    valid_mask = (places[None, :] < doc_bounds[:, -1:]).astype(jnp.float32)
    return (segment, valid_mask)


def shards(
    residual,
    out_grad,
    doc_bounds,
    norm_gain,
    proj_gate,
    proj_value,
    proj_state,
    proj_step,
    conv_value,
    conv_value_bias,
    conv_state,
    conv_state_bias,
    step_bias,
    rate_log,
    skip_gain,
    skip_proj,
    mixer_gain,
    proj_out,
):
    local_len, row_count, model_width = residual.shape
    model_parts = lax.axis_size("mp")
    length = local_len * model_parts
    head_count = rate_log.shape[0]
    chan_local = proj_value.shape[1]
    head_width = chan_local // head_count
    inner_total = chan_local * model_parts
    segment, valid_mask = segments_of(doc_bounds, length)
    wide_in = residual.astype(jnp.float32)
    scale_in = lax.rsqrt(jnp.mean(wide_in * wide_in, -1, keepdims=True) + epsilon)
    normed = (wide_in * scale_in * norm_gain).astype(jnp.bfloat16)
    normed_full = lax.all_gather(normed, "mp", axis=0, tiled=True)

    def project(weight_in):
        return jnp.moveaxis(
            jnp.dot(normed_full, weight_in, preferred_element_type=jnp.float32), 1, 0
        )

    gate_pre = project(proj_gate)
    value_pre = project(proj_value)
    step_pre = project(proj_step)
    state_pre = project(proj_state)

    def front_row(row_data):
        value_row, state_row, step_row, seg_row = row_data
        value_act, state_act = conv_silu(
            value_row, state_row, conv_value, conv_value_bias, conv_state, conv_state_bias, seg_row
        )
        value_low = value_act.astype(jnp.bfloat16)
        state_low = state_act.astype(jnp.bfloat16)
        scanned = quasiseparable(
            value_low.astype(jnp.float32).reshape(length, head_count, head_width),
            state_low.astype(jnp.float32),
            step_row,
            step_bias,
            rate_log,
            seg_row,
        )
        return (value_low, state_low, scanned)

    value_low, state_low, scanned = lax.map(front_row, (value_pre, state_pre, step_pre, segment))
    skip_part = jnp.dot(value_low, skip_proj, preferred_element_type=jnp.float32)
    skip_own = lax.psum_scatter(
        skip_part.astype(jnp.bfloat16), "mp", scatter_dimension=2, tiled=True
    ).astype(jnp.float32)
    skip_coef = skip_own + skip_gain
    heads_view = value_low.reshape(row_count, length, head_count, head_width).astype(jnp.float32)
    mixed = (scanned + skip_coef[..., None] * heads_view).reshape(row_count, length, chan_local)
    gate_act = jax.nn.silu(gate_pre)
    gated = mixed * gate_act * valid_mask[..., None]
    square_sum = lax.psum(jnp.sum(gated * gated, -1), "mp")
    out_scale = lax.rsqrt(square_sum / inner_total + epsilon)[..., None]
    normed_out = jnp.moveaxis((gated * out_scale * mixer_gain).astype(jnp.bfloat16), 0, 1)
    branch = lax.psum_scatter(
        jnp.dot(normed_out, proj_out, preferred_element_type=jnp.float32).astype(jnp.bfloat16),
        "mp",
        scatter_dimension=0,
        tiled=True,
    ).astype(jnp.float32)
    output = (wide_in + branch).astype(jnp.bfloat16)
    grad_full = lax.all_gather(out_grad, "mp", axis=0, tiled=True)
    grad_proj_out = jnp.einsum(
        "lri,lrd->id", normed_out, grad_full, preferred_element_type=jnp.float32
    )
    grad_normed_out = jnp.moveaxis(
        jnp.dot(grad_full, proj_out.T, preferred_element_type=jnp.float32), 1, 0
    )
    weighted_grad = grad_normed_out * mixer_gain
    cross_sum = lax.psum(jnp.sum(weighted_grad * gated, -1), "mp")
    grad_mixer_gain = jnp.sum(grad_normed_out * gated * out_scale, (0, 1))
    cube_scale = out_scale * out_scale * out_scale
    grad_gated = (
        out_scale * weighted_grad - gated * cube_scale * (cross_sum / inner_total)[..., None]
    )
    gate_sig = jax.nn.sigmoid(gate_pre)
    grad_mixed = grad_gated * gate_act * valid_mask[..., None]
    grad_gate = (
        grad_gated * mixed * valid_mask[..., None] * gate_sig * (1.0 + gate_pre * (1.0 - gate_sig))
    )
    grad_heads = grad_mixed.reshape(row_count, length, head_count, head_width)
    grad_skip_own = jnp.sum(grad_heads * heads_view, -1)
    grad_skip_gain = jnp.sum(grad_skip_own, (0, 1))
    grad_skip_all = lax.all_gather(
        grad_skip_own.astype(jnp.bfloat16), "mp", axis=2, tiled=True
    ).astype(grad_skip_own.dtype)
    skip_wide = skip_proj.astype(jnp.float32)
    grad_direct = (grad_heads * skip_coef[..., None]).reshape(
        row_count, length, chan_local
    ) + jnp.dot(grad_skip_all, skip_wide.T, precision=highest)
    grad_skip_proj = jnp.einsum(
        "rli,rlh->ih",
        heads_view.reshape(row_count, length, chan_local),
        grad_skip_all,
        precision=highest,
    )

    def back_row(row_data):
        (
            value_row,
            state_row,
            step_row,
            seg_row,
            value_keep,
            state_keep,
            grad_scan_row,
            grad_direct_row,
        ) = row_data

        def scan_piece(value_f, state_f, step_f, bias_f, rate_f):
            return quasiseparable(
                value_f.reshape(length, head_count, head_width),
                state_f,
                step_f,
                bias_f,
                rate_f,
                seg_row,
            )

        scan_out, scan_pull = jax.vjp(
            scan_piece,
            value_keep.astype(jnp.float32),
            state_keep.astype(jnp.float32),
            step_row,
            step_bias,
            rate_log,
        )
        grad_value_scan, grad_state_act, grad_step_row, grad_bias_row, grad_rate_row = scan_pull(
            grad_scan_row
        )

        def conv_piece(value_in, state_in, kernel_v, offset_v, kernel_s, offset_s):
            return conv_silu(value_in, state_in, kernel_v, offset_v, kernel_s, offset_s, seg_row)

        conv_out, conv_pull = jax.vjp(
            conv_piece,
            value_row,
            state_row,
            conv_value,
            conv_value_bias,
            conv_state,
            conv_state_bias,
        )
        conv_grads = conv_pull((grad_value_scan + grad_direct_row, grad_state_act))
        return (grad_step_row, grad_bias_row, grad_rate_row) + tuple(conv_grads)

    (
        grad_step_rows,
        grad_bias_rows,
        grad_rate_rows,
        grad_value_rows,
        grad_state_rows,
        grad_kernel_v,
        grad_offset_v,
        grad_kernel_s,
        grad_offset_s,
    ) = lax.map(
        back_row,
        (value_pre, state_pre, step_pre, segment, value_low, state_low, grad_heads, grad_direct),
    )
    grad_step_bias = jnp.sum(grad_bias_rows, 0)
    grad_rate_log = jnp.sum(grad_rate_rows, 0)
    grad_conv_value = jnp.sum(grad_kernel_v, 0)
    grad_conv_value_bias = jnp.sum(grad_offset_v, 0)
    grad_conv_state = jnp.sum(grad_kernel_s, 0)
    grad_conv_state_bias = jnp.sum(grad_offset_s, 0)
    grad_gate_low = jnp.moveaxis(grad_gate.astype(jnp.bfloat16), 0, 1)
    grad_value_low = jnp.moveaxis(grad_value_rows.astype(jnp.bfloat16), 0, 1)
    grad_step_low = jnp.moveaxis(grad_step_rows.astype(jnp.bfloat16), 0, 1)
    grad_state_wide = jnp.moveaxis(grad_state_rows, 0, 1)
    grad_proj_gate = jnp.einsum(
        "lrd,lrc->dc", normed_full, grad_gate_low, preferred_element_type=jnp.float32
    )
    grad_proj_value = jnp.einsum(
        "lrd,lrc->dc", normed_full, grad_value_low, preferred_element_type=jnp.float32
    )
    grad_proj_step = jnp.einsum(
        "lrd,lrc->dc", normed_full, grad_step_low, preferred_element_type=jnp.float32
    )
    grad_proj_state = jnp.einsum(
        "lrd,lrc->dc", normed_full.astype(jnp.float32), grad_state_wide, precision=highest
    )
    state_weight = proj_state.astype(jnp.float32)
    term_sum = jnp.dot(grad_gate_low, proj_gate.T, preferred_element_type=jnp.float32)
    term_sum = term_sum + jnp.dot(grad_value_low, proj_value.T, preferred_element_type=jnp.float32)
    term_sum = term_sum + jnp.dot(grad_step_low, proj_step.T, preferred_element_type=jnp.float32)
    grad_normed = lax.psum_scatter(
        (term_sum + jnp.dot(grad_state_wide, state_weight.T, precision=highest)).astype(
            jnp.bfloat16
        ),
        "mp",
        scatter_dimension=0,
        tiled=True,
    ).astype(jnp.float32)
    gained = grad_normed * norm_gain
    cube_in = scale_in * scale_in * scale_in
    grad_residual = (
        out_grad.astype(jnp.float32)
        + scale_in * gained
        - wide_in * cube_in * jnp.mean(gained * wide_in, -1, keepdims=True)
    )
    grad_norm_gain = jnp.sum(grad_normed * wide_in * scale_in, (0, 1))
    shared_sums = lax.psum(
        (grad_norm_gain, grad_proj_state, grad_conv_state, grad_conv_state_bias), ("dp", "mp")
    )
    joined = (
        lax.psum(grad_proj_gate.astype(jnp.bfloat16), "dp").astype(jnp.float32),
        lax.psum(grad_proj_value.astype(jnp.bfloat16), "dp").astype(jnp.float32),
        lax.psum(grad_proj_step.astype(jnp.bfloat16), "dp").astype(jnp.float32),
        lax.psum(grad_conv_value.astype(jnp.bfloat16), "dp").astype(jnp.float32),
        lax.psum(grad_conv_value_bias.astype(jnp.bfloat16), "dp").astype(jnp.float32),
        lax.psum(grad_step_bias.astype(jnp.bfloat16), "dp").astype(jnp.float32),
        lax.psum(grad_rate_log.astype(jnp.bfloat16), "dp").astype(jnp.float32),
        lax.psum(grad_skip_gain.astype(jnp.bfloat16), "dp").astype(jnp.float32),
        lax.psum(grad_skip_proj.astype(jnp.bfloat16), "dp").astype(jnp.float32),
        lax.psum(grad_proj_out.astype(jnp.bfloat16), "dp").astype(jnp.float32),
        lax.psum(grad_mixer_gain.astype(jnp.bfloat16), "dp").astype(jnp.float32),
    )
    return (
        output,
        grad_residual,
        shared_sums[0],
        joined[0],
        joined[1],
        shared_sums[1],
        joined[2],
        joined[3],
        joined[4],
        shared_sums[2],
        shared_sums[3],
        joined[5],
        joined[6],
        joined[7],
        joined[8],
        joined[10],
        joined[9],
    )


def solution(mesh):
    return jax.shard_map(
        shards,
        mesh=mesh,
        in_specs=(
            P("mp", "dp", None),
            P("mp", "dp", None),
            P("dp", None),
            P(),
            P(None, "mp"),
            P(None, "mp"),
            P(),
            P(None, "mp"),
            P(None, "mp"),
            P("mp"),
            P(),
            P(),
            P("mp"),
            P("mp"),
            P("mp"),
            P("mp", None),
            P("mp"),
            P("mp", None),
        ),
        out_specs=(
            P("mp", "dp", None),
            P("mp", "dp", None),
            P(),
            P(None, "mp"),
            P(None, "mp"),
            P(),
            P(None, "mp"),
            P(None, "mp"),
            P("mp"),
            P(),
            P(),
            P("mp"),
            P("mp"),
            P("mp"),
            P("mp", None),
            P("mp"),
            P("mp", None),
        ),
        check_vma=False,
    )
```

profile of v0, /device:TPU:0, one launch (start us, length us, event | category | flops | bytes accessed | tf_op | source)
XLA Modules:
  0.0 2471.0 jit_solution(12825302937387764521)
XLA Ops:
  30.9 67.8 %all-gather.5.cloned.1.call-done = bf16[4096,1,768]{2,0,1:T(8,128)(2,1)} async-done(((bf16[2048,1,768]{2,0,1:T(8,128)(2,1)}), bf16[4096,1,768]{2,0,1:T(8,128)(2,1)}) %all-gather.5.cloned.1.call-update) | async-done | bytes 6291472 | tf_op jit(solution)/shard_map/all_gather | solution.py:145
  273.9 32.9 %fusion.27 = f32[32,12,64,64]{3,2,1,0:T(8,128)S(1)} fusion(f32[32,128,12,64]{1,0,3,2:T(8,128)} %bitcast.564, f32[32,128,12]{1,2,0:T(8,128)S(1)} %get-tuple-element.304, f32[32,128,64]{1,2,0:T(8,128)S(1)} %copy-done.12, f32[32,128,12]{1,2,0:T(8,128)S(1)} %copy.383), kind=kOutput, calls=%fused_computation.37 | convolution fusion | flops 2422210560 | bytes 20316160 | tf_op jit(solution)/shard_map/while/body/eval_jaxpr/chj,cjn,cjhp->chpn/dot_general | solution.py:48
  416.5 28.6 %fusion.7 = f32[32,12,128,128]{3,1,2,0:T(8,128)} fusion(f32[32,12,128,128]{3,2,1,0:T(8,128)} %get-tuple-element.310), kind=kOutput, calls=%fused_computation.6 | output fusion | flops 799014912 | bytes 50331648 | tf_op jit(solution)/shard_map/while/body/eval_jaxpr/jit(cumsum)/reduce_window_sum | solution.py:25
  445.2 28.3 %fusion.5 = f32[32,12,128,128]{3,1,2,0:T(8,128)} fusion(f32[32,12,128,128]{3,2,1,0:T(8,128)} %get-tuple-element.311), kind=kOutput, calls=%fused_computation.4 | output fusion | flops 799014912 | bytes 50331648 | tf_op jit(solution)/shard_map/while/body/eval_jaxpr/jit(cumsum)/reduce_window_sum | solution.py:25
  711.0 30.5 %fusion.365 = (f32[768]{0:T(1024)}, f32[4096,768]{0,1:T(8,128)}, f32[4096,768]{0,1:T(8,128)}, bf16[4096,768]{0,1:T(8,128)(2,1)}) fusion(bf16[4096,768]{0,1:T(8,128)(2,1)} %get-tuple-element.271, f32[4096]{0:T(1024)S(1)} %copy-done.125, f32[4096,768]{0,1:T(8,128)} %get-tuple-element.328, f32[4096]{0:T(1024)S(1)} %bitcast.655, ...), kind=kLoop, calls=%fused_computation.435 | loop fusion | flops 69205248 | bytes 88152064 | tf_op jit(solution)/shard_map/reduce_sum | solution.py:215
  804.4 35.9 %fusion.273 = f32[12,32,32]{2,1,0:T(8,128)} fusion(f32[32,12,64,64]{3,2,1,0:T(8,128)} %copy-done.6, f32[12,64,64,32]{2,1,0,3:T(8,128)} %pad_bitcast_fusion.1, f32[32,32]{1,0:T(8,128)S(1)} %copy-done.97, pred[32,32]{1,0:T(8,128)(4,1)S(1)} %copy-done.109, f32[12,32,32]{2,0,1:T(8,128)S(1)} %copy-done.55), kind=kOutput, calls=%fused_computation.280 | convolution fusion | flops 604028928 | bytes 12686336 | tf_op jit(solution)/shard_map/while/body/eval_jaxpr/transpose(jvp(hcd,dhpn->chpn))/dot_general | solution.py:52
  871.3 42.1 %fusion.190 = bf16[32,12,64,128]{3,2,1,0:T(8,128)(2,1)} fusion(f32[32,128,12,64]{1,0,3,2:T(8,128)} %bitcast.573, f32[32,128,128]{2,1,0:T(8,128)S(1)} %copy-done.27, pred[32,128,128]{2,1,0:T(8,128)(4,1)} %get-tuple-element.312, f32[32,12,128,128]{3,1,2,0:T(8,128)} %fusion.7, pred[128,128]{1,0:T(8,128)(4,1)S(1)} %copy-done.112), kind=kOutput, calls=%fused_computation.245 | convolution fusion | flops 830472192 | bytes 46678016 | tf_op jit(solution)/shard_map/while/body/eval_jaxpr/transpose(jvp(chij,cjhp->cihp))/dot_general | solution.py:17
  980.5 35.8 %fusion.278 = f32[12,32,32]{2,1,0:T(8,128)} fusion(f32[32,12,64,64]{3,2,1,0:T(8,128)} %copy-done.5, f32[12,64,64,32]{2,1,0,3:T(8,128)} %pad_bitcast_fusion, f32[32,32]{1,0:T(8,128)S(1)} %copy-done.95, pred[32,32]{1,0:T(8,128)(4,1)S(1)} %copy-done.110, f32[12,32,32]{2,0,1:T(8,128)S(1)} %copy-done.53), kind=kOutput, calls=%fused_computation.281 | convolution fusion | flops 604028928 | bytes 12686336 | tf_op jit(solution)/shard_map/while/body/eval_jaxpr/transpose(jvp(hcd,dhpn->chpn))/dot_general | solution.py:52
  1075.4 42.6 %fusion.69 = bf16[32,12,64,128]{3,2,1,0:T(8,128)(2,1)} fusion(f32[32,12,64,128]{3,0,2,1:T(8,128)} %bitcast.592, f32[32,128,128]{2,1,0:T(8,128)S(1)} %copy-done.63, pred[32,128,128]{2,1,0:T(8,128)(4,1)S(1)} %copy-done.82, f32[32,12,128,128]{3,1,2,0:T(8,128)} %fusion.5, pred[128,128]{1,0:T(8,128)(4,1)S(1)} %copy-done.113), kind=kOutput, calls=%fused_computation.128 | convolution fusion | flops 830472192 | bytes 46678016 | tf_op jit(solution)/shard_map/while/body/eval_jaxpr/transpose(jvp(chij,cjhp->cihp))/dot_general | solution.py:17
  1248.3 70.4 %fusion.12 = (bf16[32,128,128]{2,1,0:T(8,128)(2,1)}, bf16[32,128,128]{2,1,0:T(8,128)(2,1)}, f32[32,12,128,128]{3,2,1,0:T(8,128)}, f32[32,12,128,128]{3,2,1,0:T(8,128)}) fusion(pred[32,128,128]{2,1,0:T(8,128)(4,1)} %get-tuple-element.313, f32[32,12,128,128]{3,1,2,0:T(8,128)} %fusion.5, pred[128,128]{1,0:T(8,128)(4,1)S(1)} %copy-done.113, ...), kind=kOutput, calls=%fused_computation.15 | convolution fusion | flops 917504000 | bytes 139476992 | tf_op jit(solution)/shard_map/while/body/eval_jaxpr/transpose(jvp(chij,cjhp->cihp))/dot_general | solution.py:17
  1419.5 40.4 %reduce_window_sum.136 = f32[32,12,128]{2,1,0:T(8,128)} reduce-window(f32[32,12,128]{2,1,0:T(8,128)S(1)} %fusion.311, f32[]{:T(128)} %constant.173.clone.1), window={size=1x1x128 pad=0_0x0_0x0_127}, to_apply=%region_20.21 | reduce-window | flops 6242304 | bytes 393220 | tf_op jit(solution)/shard_map/while/body/eval_jaxpr/transpose(jvp(jit(cumsum)))/reduce_window_sum | solution.py:46
  1459.9 86.7 %fusion.1 = f32[32,12,128,128]{3,1,2,0:T(8,128)} fusion(f32[32,12,128,128]{3,2,1,0:T(8,128)} %get-tuple-element.275), kind=kOutput, calls=%fused_computation | output fusion | flops 799014912 | bytes 50331648 | tf_op jit(solution)/shard_map/while/body/eval_jaxpr/transpose(jvp(jit(cumsum)))/reduce_window_sum | solution.py:25
  1546.6 32.8 %fusion.38 = (f32[32,128,64]{1,2,0:T(8,128)}, f32[32,12,64,128]{3,2,1,0:T(8,128)}) fusion(f32[32,128,12]{1,2,0:T(8,128)} %copy-done.32, f32[32,12,64,64]{2,3,1,0:T(8,128)} %copy.461, f32[32,128,12,64]{1,0,3,2:T(8,128)} %bitcast.567, f32[32,128,12]{1,2,0:T(8,128)S(1)} %copy-done.22), kind=kOutput, calls=%fused_computation.64 | convolution fusion | flops 2425094144 | bytes 32899072 | tf_op jit(solution)/shard_map/while/body/eval_jaxpr/transpose(jvp(chj,cjn,cjhp->chpn))/dot_general | solution.py:48
  1579.5 37.3 %fusion.44 = (f32[32,128,12]{1,2,0:T(8,128)}, f32[32,12,64,128]{3,2,1,0:T(8,128)}) fusion(f32[32,128,12,64]{1,0,3,2:T(8,128)S(1)} %bitcast.570, bf16[32,12,64,128]{3,2,1,0:T(8,128)(2,1)} %fusion.190, f32[32,12,64,64]{2,3,1,0:T(8,128)} %copy.461, f32[32,128,12]{1,2,0:T(8,128)S(1)} %copy-done.33, f32[32,128,64]{1,2,0:T(8,128)S(1)} %copy-done.13), kind=kOutput, calls=%fused_computation.75 | convolution fusion | flops 2431598592 | bytes 39190528 | tf_op jit(solution)/shard_map/while/body/eval_jaxpr/transpose(jvp(chj,cjn,cjhp->chpn))/dot_general | solution.py:48
  1630.7 41.0 %reduce_window_sum.139 = f32[32,12,128]{2,1,0:T(8,128)} reduce-window(f32[32,12,128]{2,1,0:T(8,128)} %fusion.307, f32[]{:T(128)} %constant.173.clone.1), window={size=1x1x128 pad=0_0x0_0x0_127}, to_apply=%region_26.27 | reduce-window | flops 6242304 | bytes 393220 | tf_op jit(solution)/shard_map/while/body/eval_jaxpr/transpose(jvp(jit(cumsum)))/reduce_window_sum | solution.py:46
  1702.3 42.1 %multiply_reduce_fusion.6 = (f32[768]{0:T(1024)S(1)}, f32[4096,768]{0,1:T(8,128)}, f32[768]{0:T(1024)S(1)}, f32[4096,768]{0,1:T(8,128)}, f32[768]{0:T(1024)S(1)}, /*index=5*/f32[4096,768]{0,1:T(8,128)}, f32[4096,768]{0,1:T(8,128)}) fusion(f32[4093,768]{0,1:T(8,128)} %bitcast.561, f32[4096]{0:T(1024)S(1)} %copy-done.84, f32[4095,768]{0,1:T(8,128)} %bitcast.563, ...), kind=kOutput, calls=%fused_computation.101 | convolution fusion | flops 217052928 | bytes 126299136 | tf_op jit(solution)/shard_map/dot_general | solution.py:222
  1818.1 86.5 %fusion.3 = f32[32,12,128,128]{3,1,2,0:T(8,128)} fusion(f32[32,12,128,128]{3,2,1,0:T(8,128)} %get-tuple-element.276), kind=kOutput, calls=%fused_computation.2 | output fusion | flops 799014912 | bytes 50331648 | tf_op jit(solution)/shard_map/while/body/eval_jaxpr/transpose(jvp(jit(cumsum)))/reduce_window_sum | solution.py:25
  1904.7 30.2 %fusion.18 = (f32[32,12,128]{2,1,0:T(8,128)S(1)}, f32[32,12,128]{2,1,0:T(8,128)S(1)}) fusion(f32[32,12,128,128]{3,1,2,0:T(8,128)} %fusion.3, pred[128,128]{1,0:T(8,128)(4,1)S(1)} %copy-done.93, f32[32,12,128,128]{3,1,2,0:T(8,128)} %fusion.1), kind=kLoop, calls=%fused_computation.23 | loop fusion | flops 25067520 | bytes 50741248 | tf_op jit(solution)/shard_map/while/body/eval_jaxpr/transpose(jvp())/reduce_sum | solution.py:23
  2065.2 102.3 %all-reduce.53.cloned.1.call-done = (bf16[768,768]{1,0:T(8,128)(2,1)}, bf16[768,768]{1,0:T(8,128)(2,1)}, bf16[768,768]{1,0:T(8,128)(2,1)}) async-done(((bf16[768,768]{1,0:T(8,128)(2,1)}, bf16[768,768]{1,0:T(8,128)(2,1)}, bf16[768,768]{1,0:T(8,128)(2,1)}), (bf16[768,768]{1,0:T(8,128)(2,1)}, bf16[768,768]{1,0:T(8,128)(2,1)}, bf16[768,768]{1,0:T(8,128)(2,1)})) %all-reduce.53.cloned.1.call-update) | async-done | bytes 3538960 | tf_op jit(solution)/shard_map/psum | solution.py:339
  2176.2 70.4 %reduce-scatter.8.cloned.1.call-done = bf16[2048,1,768]{2,0,1:T(8,128)(2,1)} async-done(((bf16[4096,1,768]{2,0,1:T(8,128)(2,1)}), bf16[2048,1,768]{2,0,1:T(8,128)(2,1)}) %reduce-scatter.8.cloned.1.call-update) | async-done | bytes 3145744 | tf_op jit(solution)/shard_map/reduce_scatter | solution.py:319
  2251.3 74.7 %reduce-scatter.6.cloned.1.call-done = bf16[2048,1,768]{2,0,1:T(8,128)(2,1)} async-done(((bf16[4096,1,768]{2,0,1:T(8,128)(2,1)}), bf16[2048,1,768]{2,0,1:T(8,128)(2,1)}) %reduce-scatter.6.cloned.1.call-update) | async-done | bytes 3145744 | tf_op jit(solution)/shard_map/reduce_scatter | solution.py:187
  2333.1 34.9 %copy.477 = f32[2048,1,768]{2,1,0:T(1,128)} copy(f32[2048,1,768]{2,0,1:T(8,128)S(1)} %get-tuple-element.288) | data formatting | bytes 12582912
  2368.0 39.4 %all-reduce.42 = (f32[768]{0:T(1024)}, f32[4,256]{1,0:T(4,128)}, f32[256]{0:T(256)}) all-reduce(f32[768]{0:T(1024)S(1)} %get-tuple-element.220, f32[4,256]{1,0:T(4,128)S(1)} %pad_add_fusion.1, f32[256]{0:T(256)S(1)} %get-tuple-element.222), channel_id=1, replica_groups=mesh['dp'=16,'mp'=2] {'dp','mp'}, use_global_device_ids=true, to_apply=%region_34.35 | all-reduce | flops 2048 | bytes 16384 | tf_op jit(solution)/shard_map/psum | solution.py:335
  2407.4 54.3 %all-reduce.49.cloned.1.call-done = f32[768,256]{1,0:T(8,128)} async-done(((f32[768,256]{1,0:T(8,128)}), f32[768,256]{1,0:T(8,128)}) %all-reduce.49.cloned.1.call-update) | async-done | bytes 786448 | tf_op jit(solution)/shard_map/psum | solution.py:335
  (613 shorter events, 1265.6 us)
Async XLA Ops:
  7.2 656.6 %copy-start = (bf16[768,768]{1,0:T(8,128)(2,1)S(1)}, bf16[768,768]{1,0:T(8,128)(2,1)}, u32[]{:S(2)}) copy-start(bf16[768,768]{1,0:T(8,128)(2,1)} %param.22) | copy-start | bytes 3538948
  7.3 91.5 %all-gather.5.cloned.1.call-start = ((), (), s32[]{:S(2)}) async-start(), calls=%async_computation.2 | async-start | bytes 9437184 | tf_op jit(solution)/shard_map/all_gather | solution.py:145
  15.6 115.3 %copy-start.68 = (bf16[768,256]{1,0:T(8,128)(2,1)S(1)}, bf16[768,256]{1,0:T(8,128)(2,1)}, u32[]{:S(2)}) copy-start(bf16[768,256]{1,0:T(8,128)(2,1)} %param.24) | copy-start | bytes 1179652
  15.6 672.9 %all-gather.7.cloned.1.call-start = ((), (), s32[]{:S(2)}) async-start(), calls=%async_computation.4 | async-start | bytes 9437184 | tf_op jit(solution)/shard_map/all_gather | solution.py:194
  16.3 2038.8 %all-reduce.51.cloned.1.call-start = ((), (), s32[]{:S(2)}) async-start(), calls=%async_computation.7 | async-start | bytes 171008 | tf_op jit(solution)/shard_map/psum | solution.py:341
  19.1 89.6 %copy-start.91 = (pred[128,128]{1,0:T(8,128)(4,1)}, pred[128,128]{1,0:T(8,128)(4,1)S(1)}, u32[]{:S(2)}) copy-start(pred[128,128]{1,0:T(8,128)(4,1)S(1)} %iota_compare_fusion.1) | copy-start | bytes 49156
  30.9 104.7 %copy-start.85 = (f32[4096]{0:T(1024)}, f32[4096]{0:T(1024)S(1)}, u32[]{:S(2)}) copy-start(f32[4096]{0:T(1024)S(1)} %get-tuple-element.316) | copy-start | bytes 49156
  30.9 104.7 %copy-start.88 = (f32[4096]{0:T(1024)}, f32[4096]{0:T(1024)S(1)}, u32[]{:S(2)}) copy-start(f32[4096]{0:T(1024)S(1)} %get-tuple-element.318) | copy-start | bytes 49156
  30.9 176.3 %copy-start.83 = (f32[4096]{0:T(1024)}, f32[4096]{0:T(1024)S(1)}, u32[]{:S(2)}) copy-start(f32[4096]{0:T(1024)S(1)} %get-tuple-element.317) | copy-start | bytes 49156
  172.2 379.9 %copy-start.20 = (f32[32,128,12]{1,2,0:T(8,128)}, f32[32,128,12]{1,2,0:T(8,128)S(1)}, u32[]{:S(2)}) copy-start(f32[32,128,12]{1,2,0:T(8,128)S(1)} %copy.383) | copy-start | bytes 589828
  247.3 398.3 %collective-permute-start = (bf16[4096,4]{0,1:T(4,128)(2,1)}, bf16[4096,4]{0,1:T(4,128)(2,1)}, u32[]{:S(2)}, u32[]{:S(2)}) collective-permute-start(bf16[4096,4]{0,1:T(4,128)(2,1)} %slice.307), channel_id=1, source_target_pairs={{0,1},{2,3},{4,5},{6,7},{8,9},{10,11},{12,13},{14,15},{16,17},{18,... | collective-permute-start | bytes 98312
  350.9 413.4 %copy-start.40 = (f32[32,128,12]{1,2,0:T(8,128)}, f32[32,128,12]{1,2,0:T(8,128)S(1)}, u32[]{:S(2)}) copy-start(f32[32,128,12]{1,2,0:T(8,128)S(1)} %get-tuple-element.307) | copy-start | bytes 589828
  1248.3 86.6 %copy-start.41 = (f32[32,128,12]{1,2,0:T(8,128)S(1)}, f32[32,128,12]{1,2,0:T(8,128)}, u32[]{:S(2)}) copy-start(f32[32,128,12]{1,2,0:T(8,128)} %copy-done.40) | copy-start | bytes 589828
  1459.9 86.7 %copy-start.22 = (f32[32,128,12]{1,2,0:T(8,128)S(1)}, f32[32,128,12]{1,2,0:T(8,128)}, u32[]{:S(2)}) copy-start(f32[32,128,12]{1,2,0:T(8,128)} %copy-done.20) | copy-start | bytes 589828
  1459.9 119.6 %slice-start = ((s8[12582912]{0:T(1024)(128)(4,1)}), s8[4194304]{0:T(1024)(128)(4,1)S(1)}, s32[]{:S(2)}) async-start(s8[12582912]{0:T(1024)(128)(4,1)} %bitcast.568), calls=%async_computation.9 | async-start | bytes 8388608
  1459.9 119.6 %slice-start.1 = ((s8[12582912]{0:T(1024)(128)(4,1)}), s8[4194304]{0:T(1024)(128)(4,1)S(1)}, s32[]{:S(2)}) async-start(s8[12582912]{0:T(1024)(128)(4,1)} %bitcast.568), calls=%async_computation.10 | async-start | bytes 8388608
  1966.4 201.2 %all-reduce.53.cloned.1.call-start = ((), (), s32[]{:S(2)}) async-start(), calls=%async_computation.8 | async-start | bytes 7077888 | tf_op jit(solution)/shard_map/psum | solution.py:339
  2000.3 246.3 %reduce-scatter.8.cloned.1.call-start = ((), (), s32[]{:S(2)}) async-start(), calls=%async_computation.5 | async-start | bytes 9437184 | tf_op jit(solution)/shard_map/reduce_scatter | solution.py:319
  2022.7 303.3 %reduce-scatter.6.cloned.1.call-start = ((), (), s32[]{:S(2)}) async-start(), calls=%async_computation.3 | async-start | bytes 9437184 | tf_op jit(solution)/shard_map/reduce_scatter | solution.py:187
  2035.3 211.4 %copy-start.124 = (f32[2048]{0:T(1024)S(1)}, f32[2048]{0:T(1024)}, u32[]{:S(2)}) copy-start(f32[2048]{0:T(1024)} %copy-done.123) | copy-start | bytes 24580
  2035.3 211.4 %copy-start.130 = (f32[768]{0:T(1024)S(1)}, f32[768]{0:T(1024)}, u32[]{:S(2)}) copy-start(f32[768]{0:T(1024)} %param.21) | copy-start | bytes 9220
  2035.3 290.7 %copy-start.137 = (f32[2048]{0:T(1024)S(1)}, f32[2048]{0:T(1024)}, u32[]{:S(2)}) copy-start(f32[2048]{0:T(1024)} %get-tuple-element.319) | copy-start | bytes 24580
  2035.3 426.4 %all-reduce.49.cloned.1.call-start = ((), (), s32[]{:S(2)}) async-start(), calls=%async_computation.6 | async-start | bytes 1572864 | tf_op jit(solution)/shard_map/psum | solution.py:335
  2326.0 137.8 %copy-start.1 = (bf16[768,768]{1,0:T(8,128)(2,1)S(1)}, bf16[768,768]{1,0:T(8,128)(2,1)}, u32[]{:S(2)}) copy-start(bf16[768,768]{1,0:T(8,128)(2,1)} %param.22) | copy-start | bytes 3538948
  (170 other events, 3643.2 us)
Sparse Core Ops, SparseCore 0:
  15.7 83.0 all-gather.4
  100.3 80.3 all-gather.6
  1966.5 88.5 all-reduce.50
  2060.1 107.4 all-reduce.52
  2170.3 76.2 reduce-scatter.7
  2248.8 77.1 reduce-scatter.5
  2331.7 129.8 all-reduce.48
where the time goes:
time: 2490 us; the launch traced here: 2470 us
  matrix products  922 us (37%)
  other arithmetic  714 us (29%)
  waiting for transfers between devices  378 us (15%)
  local copies, waits for them, and re-layouts  368 us (15%)
  blocking collectives  67.4 us (3%)
    dot_general x12, matrix products, contract(): jnp.einsum(form, left_op, right_op, preferred_element_type=jnp.float32)  244 us
    another operation x8, other arithmetic, segment_sums(): running = jnp.cumsum(jnp.where(lower_mask, repeated, 0.0), axis=-2)  233 us
    dot_general x6, matrix products, scan_direction(): jnp.einsum('chj,cjn,cjhp->chpn', to_end, key_block, weighted, precision=h...  174 us
    dot_general x6, matrix products, scan_direction(): totals = jnp.einsum('hcd,dhpn->chpn', carry_mix, states, precision=highest)  147 us
    dot_general x6, matrix products, scan_direction(): jnp.einsum('cin,chpn,chi->cihp', read_block, entering, reaching, precisio...  123 us
    unnamed x391, local copies, waits for them, and re-layouts  120 us
    psum x1, waiting for transfers between devices, shards(): lax.psum(grad_proj_gate.astype(jnp.bfloat16), 'dp').astype(jnp.float32)  102 us
    another operation x4, other arithmetic, scan_direction(): running = jnp.cumsum(log_decay, axis=-1)  99.5 us
  transfers between devices with their start and end apart: 8, of which 6 were waited for; matrix products, arithmetic and copies ran while one was open for 30% of the time, Pallas kernels for 0%

commit v1 on v0

v1 whole, which is shorter than its diff:
```python
import functools

import jax
import jax.numpy as jnp
from jax import lax
from jax.experimental import pallas as pl
from jax.experimental.pallas import tpu as pltpu
from jax.sharding import PartitionSpec as P

epsilon = 1e-05
BLOCK = 128
LANES = 128
LOG2E = 1.4426950408889634
f32 = jnp.float32
bf16 = jnp.bfloat16


def mm(a, b):
    return jnp.dot(a, b, preferred_element_type=f32)


def mm_nt(a, b):
    return lax.dot_general(a, b, (((1,), (1,)), ((), ())), preferred_element_type=f32)


def mm_tn(a, b):
    return lax.dot_general(a, b, (((0,), (0,)), ((), ())), preferred_element_type=f32)


def halves(w, axis):
    high = w.astype(bf16)
    low = (w - high.astype(f32)).astype(bf16)
    return jnp.concatenate([high, low], axis)


def iotas(rows, cols):
    return (
        lax.broadcasted_iota(jnp.int32, (rows, cols), 0),
        lax.broadcasted_iota(jnp.int32, (rows, cols), 1),
    )


def sigmoid(v):
    return 0.5 + 0.5 * jnp.tanh(0.5 * v)


def triangle(upper):
    row, col = iotas(BLOCK, BLOCK)
    keep = (col >= row) if upper else (col <= row)
    ones = jnp.where(keep, 1.0, 0.0).astype(bf16)
    return jnp.concatenate([ones, ones], 1)


def block_sums(values, heads, prefix_first):
    pair = halves(values, 0)
    below = mm(triangle(False), pair)
    above = mm(triangle(True), pair)
    lane = iotas(BLOCK, LANES)[1]
    first = lane < heads
    return jnp.where(first, below, above) if prefix_first else jnp.where(first, above, below)


def mask_lanes(meta, first_col, second_col, heads):
    lane = iotas(BLOCK, LANES)[1]
    return jnp.where(lane < heads, meta[:, first_col : first_col + 1], meta[:, second_col : second_col + 1])


def decay_parts(r2, sp, meta, heads):
    q2 = r2 - jnp.log(sp) * LOG2E
    lane = iotas(1, LANES)[1]
    end_row = jnp.where(lane < heads, r2[BLOCK - 1 : BLOCK, :], r2[0:1, :])
    reach = jnp.exp2(r2) * mask_lanes(meta, 6, 7, heads)
    weigh = jnp.exp2(end_row - q2) * mask_lanes(meta, 8, 9, heads)
    return q2, reach, weigh


def front_kernel(
    heads, width, blocks,
    res, halo, meta_ref, ng, wv, ws, wst, taps, step_bias, rate, ef2, eb2,
    normed_out, x_out, g_out, u_out, c_out, rs_out, sfl, sbl, coef, fin,
    ubuf, sf, stb, dfs, dbs,
):
    c = pl.program_id(0)
    inner = wv.shape[1]
    total = taps.shape[1]

    def normalize(values):
        wide = values.astype(f32)
        scale = lax.rsqrt(jnp.mean(wide * wide, -1, keepdims=True) + epsilon)
        return (wide * scale * ng[...]).astype(bf16)

    @pl.when(c == 0)
    def _():
        tail = normalize(halo[...])
        ubuf[0:8, 0:inner] = mm(tail, wv[...])[8:16]
        ubuf[0:8, inner:total] = mm(tail, ws[...])[8:16]
        sf[...] = jnp.zeros_like(sf)

    @pl.when(c > 0)
    def _():
        ubuf[0:8, :] = ubuf[BLOCK : BLOCK + 8, :]

    normed = normalize(res[...])
    normed_out[...] = normed
    ubuf[8 : BLOCK + 8, 0:inner] = mm(normed, wv[...])
    ubuf[8 : BLOCK + 8, inner:total] = mm(normed, ws[...])
    meta = meta_ref[...]

    pre = mm(normed, wst[...]) + step_bias[...]
    sp = jnp.maximum(pre, 0.0) + jnp.log1p(jnp.exp(-jnp.abs(pre)))
    r2 = block_sums(-sp * (rate[...] * LOG2E), heads, True)
    rs_out[:, 0:LANES] = r2
    rs_out[:, LANES : 2 * LANES] = sp
    _, reach, weigh = decay_parts(r2, sp, meta, heads)
    lane = iotas(1, LANES)[1]
    dvec = jnp.where(lane < heads, reach[BLOCK - 1 : BLOCK, :], reach[0:1, :])
    drow = halves(jnp.broadcast_to(dvec, (8, LANES)), 1)
    dfs[pl.ds(c, 1), :] = mm(drow, ef2[...])[0:1]
    dbs[pl.ds(c, 1), :] = mm(drow, eb2[...])[0:1]
    wpair = halves(weigh, 1)

    masks = [meta[:, j : j + 1] for j in range(3)]

    def convolve(cols):
        value = taps[4:5, cols] + taps[0:1, cols] * ubuf[8 : BLOCK + 8, cols]
        for j in range(1, 4):
            value = value + taps[j : j + 1, cols] * (ubuf[8 - j : BLOCK + 8 - j, cols] * masks[j - 1])
        u_out[:, cols] = ubuf[8 : BLOCK + 8, cols].astype(bf16)
        c_out[:, cols] = value.astype(bf16)
        return (value * sigmoid(value)).astype(bf16)

    state = convolve(slice(inner, total))
    g_out[...] = state
    state_t = jnp.transpose(state.astype(f32)).astype(bf16)
    n = (total - inner) // 4
    bf_t, bb_t = state_t[0:n], state_t[2 * n : 3 * n]
    dfrow, dbrow = dfs[pl.ds(c, 1), :], dbs[pl.ds(c, 1), :]
    for start in range(0, inner, 256):
        cols = slice(start, start + 256)
        x = convolve(cols)
        x_out[:, cols] = x
        wide = x.astype(f32)
        xwf = (wide * mm(wpair, ef2[:, cols])).astype(bf16)
        xwb = (wide * mm(wpair, eb2[:, cols])).astype(bf16)
        sfl[0, :, cols] = sf[:, cols].astype(bf16)
        sf[:, cols] = dfrow[:, cols] * sf[:, cols] + mm(bf_t, xwf)
        stb[c, :, cols] = mm(bb_t, xwb)

    @pl.when(c == blocks - 1)
    def _():
        fin[0:n, :] = sf[...]
        one = jnp.ones((1, inner), f32)

        def down(i, carry):
            k = blocks - 1 - i
            dfk, dbk = dfs[pl.ds(k, 1), :], dbs[pl.ds(k, 1), :]
            suffix_f, suffix_b = carry
            base = pl.multiple_of(k * 8, 8)
            coef[pl.ds(base + 1, 1), :] = suffix_f
            coef[pl.ds(base + 3, 1), :] = suffix_b
            coef[pl.ds(base + 4, 1), :] = dfk
            coef[pl.ds(base + 5, 1), :] = dbk
            carried = fin[n : 2 * n, :]
            sbl[k] = carried.astype(bf16)
            fin[n : 2 * n, :] = dbk * carried + stb[k]
            return suffix_f * dfk, suffix_b * dbk

        fin[n : 2 * n, :] = jnp.zeros((n, inner), f32)
        lax.fori_loop(0, blocks, down, (one, one))

        def up(k, carry):
            dfk, dbk = dfs[pl.ds(k, 1), :], dbs[pl.ds(k, 1), :]
            prefix_f, prefix_b = carry
            base = pl.multiple_of(k * 8, 8)
            coef[pl.ds(base, 1), :] = prefix_f
            coef[pl.ds(base + 2, 1), :] = prefix_b
            coef[pl.ds(base + 6, 1), :] = prefix_f * dfk
            coef[pl.ds(base + 7, 1), :] = prefix_b * dbk
            return prefix_f * dfk, prefix_b * dbk

        lax.fori_loop(0, blocks, up, (one, one))


def masked_scores(state, segrow, meta, n):
    bf, cf = state[:, 0:n], state[:, n : 2 * n]
    bb, cb = state[:, 2 * n : 3 * n], state[:, 3 * n : 4 * n]
    row, col = iotas(BLOCK, BLOCK)
    lower = row > col
    same = meta[:, 11:12] == segrow
    picked = jnp.where(lower, mm_nt(cf, bf), mm_nt(cb, bb))
    keep = jnp.where(row == col, 0.0, jnp.where(same, 1.0, 0.0))
    return bf, cf, bb, cb, lower, keep, picked * keep


def decay_matrix(h, heads, r2, q_t, lower):
    forward = r2[:, h : h + 1] - q_t[h : h + 1, :]
    k = heads + h
    reverse = r2[:, k : k + 1] - q_t[k : k + 1, :]
    return jnp.exp2(jnp.where(lower, forward, reverse))


def middle_kernel(
    heads, width, blocks,
    res, og_ref, normed_ref, x_ref, g_ref, rs_ref, meta_ref, segrow_ref, sfl, sbl, coef, entry_f, entry_b,
    wg, wo, skip, skip_gain, mixer_gain, ef2, eb2, eft, lanes,
    out, no_out, ggate_out, dy_out, direct_out, dtf, dtb, dfin, dmix, dskip_w, dskip_g,
    yv, dstf, drow, gpre,
):
    c = pl.program_id(0)
    inner = x_ref.shape[1]
    n = g_ref.shape[1] // 4

    @pl.when(c == 0)
    def _():
        dmix[...] = jnp.zeros_like(dmix)
        dskip_w[...] = jnp.zeros_like(dskip_w)
        dskip_g[...] = jnp.zeros_like(dskip_g)
        dfin[...] = jnp.zeros_like(dfin)

    meta = meta_ref[...]
    r2, sp = rs_ref[:, 0:LANES], rs_ref[:, LANES : 2 * LANES]
    q2, reach, _ = decay_parts(r2, sp, meta, heads)
    q_t = jnp.transpose(q2)
    bf, cf, bb, cb, lower, _, gm = masked_scores(g_ref[...], segrow_ref[0], meta, n)
    low_half, high_half = lanes[0:1, :], lanes[1:2, :]
    state_t = jnp.transpose(g_ref[...].astype(f32)).astype(bf16)
    cf_t, cb_t = state_t[n : 2 * n], state_t[3 * n : 4 * n]
    rpair = halves(reach, 1)
    valid = meta[:, 10:11]
    x_all = x_ref[...]
    skip_coef = mm(x_all, skip[...]) + skip_gain[...]
    spair = halves(skip_coef, 1)
    gpre[...] = mm(normed_ref[...], wg[...])

    square = jnp.zeros((BLOCK, 1), f32)
    per = LANES // width
    for p in range(inner // LANES):
        cols = slice(p * LANES, (p + 1) * LANES)
        x = x_ref[:, cols]
        mixes = [
            (decay_matrix(per * p + k, heads, r2, q_t, lower) * gm).astype(bf16) for k in range(per)
        ]
        spread = jnp.concatenate([x * low_half, x * high_half], 0)
        scanned = mm(jnp.concatenate(mixes, 1), spread)
        sf_in = (sfl[0, :, cols].astype(f32) + coef[0:1, cols] * entry_f[:, cols].astype(f32)).astype(bf16)
        sb_in = (sbl[0, :, cols].astype(f32) + coef[3:4, cols] * entry_b[:, cols].astype(f32)).astype(bf16)
        scanned = scanned + mm(rpair, ef2[:, cols]) * mm(cf, sf_in) + mm(rpair, eb2[:, cols]) * mm(cb, sb_in)
        mixed = scanned + mm(spair, ef2[:, cols]) * x.astype(f32)
        yv[:, cols] = mixed
        gate = gpre[:, cols]
        gated = mixed * (gate * sigmoid(gate)) * valid
        square = square + jnp.sum(gated * gated, -1, keepdims=True)
    scale = lax.rsqrt(square * (1.0 / inner) + epsilon)

    og = og_ref[...]
    gno = mm_nt(og, wo[...])
    cross = jnp.zeros((BLOCK, 1), f32)
    for start in range(0, inner, 256):
        cols = slice(start, start + 256)
        gate = gpre[:, cols]
        gated = yv[:, cols] * (gate * sigmoid(gate)) * valid
        weighted = gno[:, cols] * mixer_gain[:, cols]
        no_out[:, cols] = (gated * scale * mixer_gain[:, cols]).astype(bf16)
        cross = cross + jnp.sum(weighted * gated, -1, keepdims=True)
        dmix[0:1, cols] += jnp.sum(gno[:, cols] * (gated * scale), 0, keepdims=True)
    out[...] = (res[...].astype(f32) + mm(no_out[...], wo[...])).astype(bf16)
    cross = cross * (scale * scale * scale) * (1.0 / inner)

    dskip = jnp.zeros((BLOCK, LANES), f32)
    for start in range(0, inner, 256):
        cols = slice(start, start + 256)
        gate = gpre[:, cols]
        sig = sigmoid(gate)
        act = gate * sig
        mixed = yv[:, cols]
        gated = mixed * act * valid
        ggated = (scale * (gno[:, cols] * mixer_gain[:, cols]) - gated * cross) * valid
        gmixed = ggated * act
        ggate_out[:, cols] = (ggated * mixed * (sig * (1.0 + gate * (1.0 - sig)))).astype(bf16)
        dy_out[:, cols] = gmixed.astype(bf16)
        dskip = dskip + mm((gmixed * x_ref[:, cols].astype(f32)).astype(bf16), eft[cols, :])
    dskip_g[0:1, :] += jnp.sum(dskip, 0, keepdims=True)
    dskip_low = dskip.astype(bf16)
    dskip_w[...] += mm_tn(x_all, dskip_low)

    for start in range(0, inner, 256):
        cols = slice(start, start + 256)
        dy = dy_out[:, cols].astype(f32)
        direct = dy * mm(spair, ef2[:, cols]) + mm_nt(dskip_low, skip[cols, :])
        direct_out[:, cols] = direct.astype(bf16)
        dstf[c, :, cols] = mm(cf_t, (dy * mm(rpair, ef2[:, cols])).astype(bf16))
        step_b = mm(cb_t, (dy * mm(rpair, eb2[:, cols])).astype(bf16))
        carried = dfin[n : 2 * n, cols]
        dtb[0, :, cols] = carried.astype(bf16)
        dfin[n : 2 * n, cols] = coef[5:6, cols] * carried + step_b
    drow[pl.ds(c, 1), :] = coef[4:5, :]

    @pl.when(c == blocks - 1)
    def _():
        def down(i, carry):
            k = blocks - 1 - i
            carried = dfin[0:n, :]
            dtf[k] = carried.astype(bf16)
            dfin[0:n, :] = drow[pl.ds(k, 1), :] * carried + dstf[k]
            return carry

        lax.fori_loop(0, blocks, down, 0)


def scan_back_kernel(
    heads, width, blocks,
    x_ref, g_ref, rs_ref, meta_ref, segrow_ref, dy_ref, direct_ref, c_ref, sfl, sbl, coef, dtf, dtb,
    entry_f, entry_b, dentry_f, dentry_b, rate, ef2, eb2, eft, ebt, lanes,
    dca_out, dbias, dhead,
    del_fh, del_fl, del_bh, del_bl, kap_f, kap_b, dyr_f, dyr_b, xw_f, xw_b, s_f, s_b, t_f, t_b, ends,
):
    c = pl.program_id(0)
    inner = x_ref.shape[1]
    total = c_ref.shape[1]
    n = g_ref.shape[1] // 4

    @pl.when(c == 0)
    def _():
        dbias[...] = jnp.zeros_like(dbias)
        dhead[...] = jnp.zeros_like(dhead)

    meta = meta_ref[...]
    r2, sp = rs_ref[:, 0:LANES], rs_ref[:, LANES : 2 * LANES]
    q2, reach, weigh = decay_parts(r2, sp, meta, heads)
    q_t = jnp.transpose(q2)
    bf, cf, bb, cb, lower, keep, gm = masked_scores(g_ref[...], segrow_ref[0], meta, n)
    low_half, high_half = lanes[0:1, :], lanes[1:2, :]
    lower_low = jnp.where(lower, 1.0, 0.0).astype(bf16)
    rpair = halves(reach, 1)
    wpair = halves(weigh, 1)
    per = LANES // width
    dg = jnp.zeros((BLOCK, BLOCK), f32)
    for p in range(inner // LANES):
        cols = slice(p * LANES, (p + 1) * LANES)
        x, dy = x_ref[:, cols], dy_ref[:, cols]
        xf, dyf = x.astype(f32), dy.astype(f32)
        dy_spread = jnp.concatenate([dy * low_half, dy * high_half], 0)
        x_spread = jnp.concatenate([x * low_half, x * high_half], 0)
        dm = mm_nt(dy_spread, x)
        lows, ups = [], []
        for k in range(per):
            decay = decay_matrix(per * p + k, heads, r2, q_t, lower)
            dg = dg + dm[k * BLOCK : (k + 1) * BLOCK] * decay
            mix = (decay * gm).astype(bf16)
            mix_low = mix * lower_low
            lows.append(mix_low)
            ups.append(mix - mix_low)
        sf_in = (sfl[0, :, cols].astype(f32) + coef[0:1, cols] * entry_f[:, cols].astype(f32)).astype(bf16)
        sb_in = (sbl[0, :, cols].astype(f32) + coef[3:4, cols] * entry_b[:, cols].astype(f32)).astype(bf16)
        tf = (dtf[0, :, cols].astype(f32) + coef[1:2, cols] * dentry_f[:, cols].astype(f32)).astype(bf16)
        tb = (dtb[0, :, cols].astype(f32) + coef[2:3, cols] * dentry_b[:, cols].astype(f32)).astype(bf16)
        s_f[:, cols], s_b[:, cols], t_f[:, cols], t_b[:, cols] = sf_in, sb_in, tf, tb
        reach_f, reach_b = mm(rpair, ef2[:, cols]), mm(rpair, eb2[:, cols])
        weigh_f, weigh_b = mm(wpair, ef2[:, cols]), mm(wpair, eb2[:, cols])
        dyr_f[:, cols] = (dyf * reach_f).astype(bf16)
        dyr_b[:, cols] = (dyf * reach_b).astype(bf16)
        xwf, xwb = (xf * weigh_f).astype(bf16), (xf * weigh_b).astype(bf16)
        xw_f[:, cols], xw_b[:, cols] = xwf, xwb
        y_f = mm(jnp.concatenate(lows, 1), x_spread) + reach_f * mm(cf, sf_in)
        y_b = mm(jnp.concatenate(ups, 1), x_spread) + reach_b * mm(cb, sb_in)
        dw_f, dw_b = weigh_f * mm(bf, tf), weigh_b * mm(bb, tb)
        dx_f = mm_tn(jnp.concatenate(lows, 0), dy_spread) + dw_f
        dx_b = mm_tn(jnp.concatenate(ups, 0), dy_spread) + dw_b
        xdx_f, xdx_b = xf * dx_f, xf * dx_b
        kap_f[:, cols] = xdx_f.astype(bf16)
        kap_b[:, cols] = xdx_b.astype(bf16)
        for delta, high, rest in ((dyf * y_f - xdx_f, del_fh, del_fl), (dyf * y_b - xdx_b, del_bh, del_bl)):
            rounded = delta.astype(bf16)
            high[:, cols] = rounded
            rest[:, cols] = (delta - rounded.astype(f32)).astype(bf16)
        through_f = coef[4:5, cols] * jnp.sum(tf.astype(f32) * sf_in.astype(f32), 0, keepdims=True)
        through_b = coef[5:6, cols] * jnp.sum(tb.astype(f32) * sb_in.astype(f32), 0, keepdims=True)
        ends[0:1, cols] = through_f + jnp.sum(xf * dw_f, 0, keepdims=True)
        ends[1:2, cols] = through_b + jnp.sum(xf * dw_b, 0, keepdims=True)
        pre = c_ref[:, cols].astype(f32)
        sig = sigmoid(pre)
        dc = (dx_f + dx_b + direct_ref[:, cols].astype(f32)) * (sig * (1.0 + pre * (1.0 - sig)))
        dca_out[:, cols] = dc.astype(bf16)
        dbias[0:1, cols] += jnp.sum(dc, 0, keepdims=True)

    dg = dg * keep
    dg_low = jnp.where(lower, dg, 0.0)
    dg_f = dg_low.astype(bf16)
    dg_b = (dg - dg_low).astype(bf16)
    d_bf = mm_tn(dg_f, cf) + mm_nt(xw_f[...], t_f[...])
    d_cf = mm(dg_f, bf) + mm_nt(dyr_f[...], s_f[...])
    d_bb = mm_tn(dg_b, cb) + mm_nt(xw_b[...], t_b[...])
    d_cb = mm(dg_b, bb) + mm_nt(dyr_b[...], s_b[...])
    d_state = jnp.concatenate([d_bf, d_cf, d_bb, d_cb], 1)
    tail = slice(inner, total)
    pre = c_ref[:, tail].astype(f32)
    sig = sigmoid(pre)
    dc = d_state * (sig * (1.0 + pre * (1.0 - sig)))
    dca_out[:, tail] = dc.astype(bf16)
    dbias[0:1, tail] += jnp.sum(dc, 0, keepdims=True)

    delta = mm(del_fh[...], eft[...]) + mm(del_bh[...], ebt[...]) + mm(del_fl[...], eft[...]) + mm(del_bl[...], ebt[...])
    kap = mm(kap_f[...], eft[...]) + mm(kap_b[...], ebt[...])
    end_pair = halves(jnp.broadcast_to(ends[0:1, :], (8, inner)), 0)
    end_f = mm(end_pair, eft[...])
    end_pair = halves(jnp.broadcast_to(ends[1:2, :], (8, inner)), 0)
    end_b = mm(end_pair, ebt[...])
    end = end_f[0:1] + end_f[8:9] + end_b[0:1] + end_b[8:9]
    dld = block_sums(delta, heads, False) + end
    phi = jnp.where(sp < 1e-3, 1.0 - 0.5 * sp, (1.0 - jnp.exp(-sp)) / jnp.maximum(sp, 1e-3))
    pull = dld * rate[...]
    dstep = kap * phi - pull * (phi * sp)
    dca_out[:, total : total + LANES] = dstep.astype(bf16)
    dhead[0:1, :] += jnp.sum(dstep, 0, keepdims=True)
    dhead[1:2, :] += jnp.sum(-pull * sp, 0, keepdims=True)


def conv_back_kernel(blocks, dca, nxt, halo, u, meta_ref, taps, dall, dtaps, buf):
    c = pl.program_id(0)
    total = u.shape[1]

    @pl.when(c == 0)
    def _():
        dtaps[...] = jnp.zeros_like(dtaps)

    masks = [meta_ref[:, 3 + j : 4 + j] for j in range(3)]
    for start in range(0, total, 256):
        cols = slice(start, start + 256)
        dc = dca[:, cols].astype(f32)
        buf[0:BLOCK, cols] = dc
        buf[BLOCK : BLOCK + 16, cols] = jnp.where(
            c == blocks - 1, halo[:, cols].astype(f32), nxt[:, cols].astype(f32)
        )
        uv = u[:, cols].astype(f32)
        grad = taps[0:1, cols] * dc
        dtaps[0:1, cols] += jnp.sum(uv * dc, 0, keepdims=True)
        for j in range(1, 4):
            moved = buf[j : BLOCK + j, cols] * masks[j - 1]
            grad = grad + taps[j : j + 1, cols] * moved
            dtaps[j : j + 1, cols] += jnp.sum(uv * moved, 0, keepdims=True)
        dall[:, cols] = grad.astype(bf16)
    dall[:, total:] = dca[:, total:]


def tail_kernel(res, og, ggate, dall, ng, wg, wrest, out, dng):
    c = pl.program_id(0)

    @pl.when(c == 0)
    def _():
        dng[...] = jnp.zeros_like(dng)

    grad = mm_nt(ggate[...], wg[...]) + mm_nt(dall[...], wrest[...])
    wide = res[...].astype(f32)
    scale = lax.rsqrt(jnp.mean(wide * wide, -1, keepdims=True) + epsilon)
    gained = grad * ng[...]
    cube = scale * scale * scale * jnp.mean(gained * wide, -1, keepdims=True)
    out[...] = og[...].astype(f32) + scale * gained - wide * cube
    dng[0:1, :] += jnp.sum(grad * (wide * scale), 0, keepdims=True)


def row_spec(rows, cols):
    return pl.BlockSpec((rows, cols), lambda c: (c, 0))


def plane_spec(rows, cols):
    return pl.BlockSpec((1, rows, cols), lambda c: (c, 0, 0))


def whole_spec(array):
    rank = len(array.shape)
    return pl.BlockSpec(tuple(array.shape), lambda c: (0,) * rank, pipeline_mode=pl.Buffered(1))


def shaped(shape, kind):
    return jax.ShapeDtypeStruct(shape, kind)


def shards(
    residual,
    out_grad,
    doc_bounds,
    norm_gain,
    proj_gate,
    proj_value,
    proj_state,
    proj_step,
    conv_value,
    conv_value_bias,
    conv_state,
    conv_state_bias,
    step_bias,
    rate_log,
    skip_gain,
    skip_proj,
    mixer_gain,
    proj_out,
):
    length, row_count, model_width = residual.shape
    assert row_count == 1 and length % BLOCK == 0
    parts = lax.axis_size("mp")
    me = lax.axis_index("mp")
    own_heads = rate_log.shape[0]
    own_chan = proj_value.shape[1]
    heads = own_heads * parts
    inner = own_chan * parts
    width = own_chan // own_heads
    state_all = proj_state.shape[1]
    n = state_all // 4
    total = inner + state_all
    blocks = length // BLOCK
    full_len = length * parts
    res = residual[:, 0, :]
    og = out_grad[:, 0, :]

    def gather(values, axis):
        return lax.all_gather(values, "mp", axis=axis, tiled=True)

    right = [(i, i + 1) for i in range(parts - 1)]
    left = [(i + 1, i) for i in range(parts - 1)]

    halo = lax.ppermute(res[length - 16 :], "mp", right)
    wv = gather(proj_value, 1)
    small = jnp.concatenate(
        [conv_value.reshape(-1), conv_value_bias, mixer_gain, step_bias, rate_log, skip_gain]
    )
    small = gather(small[None], 0)
    sizes = [4 * own_chan, own_chan, own_chan, 2 * own_heads, own_heads, own_heads]
    at, pieces = 0, []
    for size in sizes:
        pieces.append(small[:, at : at + size])
        at += size
    conv_v = jnp.moveaxis(pieces[0].reshape(parts, 4, own_chan), 0, 1).reshape(4, inner)
    bias_v, gain_m = pieces[1].reshape(1, inner), pieces[2].reshape(1, inner)

    def by_direction(values):
        lead = values.shape[:-1]
        return jnp.swapaxes(values.reshape(lead + (heads, 2)), -1, -2).reshape(lead + (2 * heads,))

    def pad_lanes(values):
        return jnp.pad(values, [(0, 0)] * (values.ndim - 1) + [(0, LANES - values.shape[-1])])

    bias_s = pad_lanes(by_direction(pieces[3].reshape(1, 2 * heads)))
    rate = pad_lanes(jnp.tile(jnp.exp(pieces[4].reshape(1, heads)), (1, 2)))
    gain_s = pad_lanes(pieces[5].reshape(1, heads))
    wst = pad_lanes(by_direction(gather(proj_step, 1)))
    skip = pad_lanes(gather(skip_proj, 0))
    wg = gather(proj_gate, 1)
    wo = gather(proj_out, 0)
    taps = jnp.concatenate(
        [
            jnp.concatenate([conv_v, conv_state], 1),
            jnp.concatenate([bias_v, conv_state_bias[None]], 1),
            jnp.zeros((3, total), f32),
        ],
        0,
    )
    ng = norm_gain[None]

    bounds = doc_bounds[0]

    def segment_at(places):
        found = jnp.sum((places[:, None] >= bounds[None, :]).astype(jnp.int32), -1)
        return jnp.where(places < 0, -1, jnp.where(places >= full_len, -2, found))

    pos = me * length + jnp.arange(length, dtype=jnp.int32)
    base = pos - pos % BLOCK
    seg = segment_at(pos)
    columns = [segment_at(pos - j) == seg for j in (1, 2, 3)]
    columns += [segment_at(pos + j) == seg for j in (1, 2, 3)]
    columns += [segment_at(base - 1) == seg, segment_at(base + BLOCK) == seg]
    columns += [segment_at(base + BLOCK - 1) == seg, segment_at(base) == seg]
    columns += [pos < bounds[-1]]
    meta = jnp.stack([v.astype(f32) for v in columns] + [seg.astype(f32)], 1)
    meta = pad_lanes(meta)
    segrow = seg.astype(f32).reshape(blocks, 1, BLOCK)

    chan_head = jnp.arange(inner) // width
    lane_id = jnp.arange(LANES)
    spread_f = (lane_id[:, None] == chan_head[None, :]).astype(bf16)
    spread_b = (lane_id[:, None] == chan_head[None, :] + heads).astype(bf16)
    ef2, eb2 = jnp.concatenate([spread_f] * 2, 0), jnp.concatenate([spread_b] * 2, 0)
    eft, ebt = spread_f.T, spread_b.T
    half = (jnp.arange(LANES) < width).astype(bf16)
    lanes = jnp.concatenate([half[None], 1 - half[None], jnp.zeros((14, LANES), bf16)], 0)

    params = pltpu.CompilerParams(dimension_semantics=("arbitrary",), vmem_limit_bytes=60 * 1024 * 1024)

    front_in = (res, halo, meta, ng, wv, proj_state, wst, taps, bias_s, rate, ef2, eb2)
    normed, x, g, u, cpre, rs, sfl, sbl, coef, fin = pl.pallas_call(
        functools.partial(front_kernel, heads, width, blocks),
        grid=(blocks,),
        in_specs=[row_spec(BLOCK, model_width), whole_spec(halo), row_spec(BLOCK, LANES)]
        + [whole_spec(v) for v in front_in[3:]],
        out_specs=[
            row_spec(BLOCK, model_width),
            row_spec(BLOCK, inner),
            row_spec(BLOCK, state_all),
            row_spec(BLOCK, total),
            row_spec(BLOCK, total),
            row_spec(BLOCK, 2 * LANES),
            plane_spec(n, inner),
            pl.BlockSpec((blocks, n, inner), lambda c: (0, 0, 0)),
            pl.BlockSpec((blocks * 8, inner), lambda c: (0, 0)),
            pl.BlockSpec((2 * n, inner), lambda c: (0, 0)),
        ],
        out_shape=[
            shaped((length, model_width), bf16),
            shaped((length, inner), bf16),
            shaped((length, state_all), bf16),
            shaped((length, total), bf16),
            shaped((length, total), bf16),
            shaped((length, 2 * LANES), f32),
            shaped((blocks, n, inner), bf16),
            shaped((blocks, n, inner), bf16),
            shaped((blocks * 8, inner), f32),
            shaped((2 * n, inner), f32),
        ],
        scratch_shapes=[
            pltpu.VMEM((BLOCK + 8, total), f32),
            pltpu.VMEM((n, inner), f32),
            pltpu.VMEM((blocks, n, inner), f32),
            pltpu.VMEM((blocks, inner), f32),
            pltpu.VMEM((blocks, inner), f32),
        ],
        compiler_params=params,
        name="front",
    )(*front_in)

    decay_f, decay_b = coef[blocks * 8 - 2 : blocks * 8 - 1], coef[blocks * 8 - 1 :]

    def chain(first, factor, pairs):
        got = lax.ppermute(first.astype(bf16), "mp", pairs)
        for _ in range(parts - 2):
            got = lax.ppermute((first + factor * got.astype(f32)).astype(bf16), "mp", pairs)
        return got

    entry_f = chain(fin[:n], decay_f, right)
    entry_b = chain(fin[n:], decay_b, left)

    middle_in = (
        res, og, normed, x, g, rs, meta, segrow, sfl, sbl, coef, entry_f, entry_b,
        wg, wo, skip, gain_s, gain_m, ef2, eb2, eft, lanes,
    )
    coef_spec = pl.BlockSpec((8, inner), lambda c: (c, 0))
    out, normed_out, ggate, dy, direct, dtf, dtb, dfin, dmix, dskip_w, dskip_g = pl.pallas_call(
        functools.partial(middle_kernel, heads, width, blocks),
        grid=(blocks,),
        in_specs=[
            row_spec(BLOCK, model_width),
            row_spec(BLOCK, model_width),
            row_spec(BLOCK, model_width),
            row_spec(BLOCK, inner),
            row_spec(BLOCK, state_all),
            row_spec(BLOCK, 2 * LANES),
            row_spec(BLOCK, LANES),
            plane_spec(1, BLOCK),
            plane_spec(n, inner),
            plane_spec(n, inner),
            coef_spec,
        ]
        + [whole_spec(v) for v in middle_in[11:]],
        out_specs=[
            row_spec(BLOCK, model_width),
            row_spec(BLOCK, inner),
            row_spec(BLOCK, inner),
            row_spec(BLOCK, inner),
            row_spec(BLOCK, inner),
            pl.BlockSpec((blocks, n, inner), lambda c: (0, 0, 0)),
            plane_spec(n, inner),
            pl.BlockSpec((2 * n, inner), lambda c: (0, 0)),
            pl.BlockSpec((8, inner), lambda c: (0, 0)),
            pl.BlockSpec((inner, LANES), lambda c: (0, 0)),
            pl.BlockSpec((8, LANES), lambda c: (0, 0)),
        ],
        out_shape=[
            shaped((length, model_width), bf16),
            shaped((length, inner), bf16),
            shaped((length, inner), bf16),
            shaped((length, inner), bf16),
            shaped((length, inner), bf16),
            shaped((blocks, n, inner), bf16),
            shaped((blocks, n, inner), bf16),
            shaped((2 * n, inner), f32),
            shaped((8, inner), f32),
            shaped((inner, LANES), f32),
            shaped((8, LANES), f32),
        ],
        scratch_shapes=[
            pltpu.VMEM((BLOCK, inner), f32),
            pltpu.VMEM((blocks, n, inner), f32),
            pltpu.VMEM((blocks, inner), f32),
            pltpu.VMEM((BLOCK, inner), f32),
        ],
        compiler_params=params,
        name="middle",
    )(*middle_in)

    dentry_f = chain(dfin[:n], decay_f, left)
    dentry_b = chain(dfin[n:], decay_b, right)

    def outer_sum(left_op, right_op):
        return lax.dot_general(left_op, right_op, (((0,), (0,)), ((), ())), preferred_element_type=f32)

    def reduce_rows(values, axis):
        mine = lax.psum_scatter(values.astype(bf16), "mp", scatter_dimension=axis, tiled=True)
        return lax.psum(mine, "dp").astype(f32)

    grad_proj_out = reduce_rows(outer_sum(normed_out, og), 0)
    grad_proj_gate = reduce_rows(outer_sum(normed, ggate), 1)

    back_in = (
        x, g, rs, meta, segrow, dy, direct, cpre, sfl, sbl, coef, dtf, dtb,
        entry_f, entry_b, dentry_f, dentry_b, rate, ef2, eb2, eft, ebt, lanes,
    )
    wide_total = total + LANES
    dca, dbias, dhead = pl.pallas_call(
        functools.partial(scan_back_kernel, heads, width, blocks),
        grid=(blocks,),
        in_specs=[
            row_spec(BLOCK, inner),
            row_spec(BLOCK, state_all),
            row_spec(BLOCK, 2 * LANES),
            row_spec(BLOCK, LANES),
            plane_spec(1, BLOCK),
            row_spec(BLOCK, inner),
            row_spec(BLOCK, inner),
            row_spec(BLOCK, total),
            plane_spec(n, inner),
            plane_spec(n, inner),
            coef_spec,
            plane_spec(n, inner),
            plane_spec(n, inner),
        ]
        + [whole_spec(v) for v in back_in[13:]],
        out_specs=[
            row_spec(BLOCK, wide_total),
            pl.BlockSpec((8, total), lambda c: (0, 0)),
            pl.BlockSpec((8, LANES), lambda c: (0, 0)),
        ],
        out_shape=[
            shaped((length, wide_total), bf16),
            shaped((8, total), f32),
            shaped((8, LANES), f32),
        ],
        scratch_shapes=[pltpu.VMEM((BLOCK, inner), bf16)] * 10
        + [pltpu.VMEM((n, inner), bf16)] * 4
        + [pltpu.VMEM((8, inner), f32)],
        compiler_params=params,
        name="scan_back",
    )(*back_in)

    halo_back = lax.ppermute(dca[:16], "mp", left)
    dall, dtaps = pl.pallas_call(
        functools.partial(conv_back_kernel, blocks),
        grid=(blocks,),
        in_specs=[
            row_spec(BLOCK, wide_total),
            pl.BlockSpec((16, wide_total), lambda c: (jnp.minimum((c + 1) * (BLOCK // 16), length // 16 - 1), 0)),
            whole_spec(halo_back),
            row_spec(BLOCK, total),
            row_spec(BLOCK, LANES),
            whole_spec(taps),
        ],
        out_specs=[row_spec(BLOCK, wide_total), pl.BlockSpec((8, total), lambda c: (0, 0))],
        out_shape=[shaped((length, wide_total), bf16), shaped((8, total), f32)],
        scratch_shapes=[pltpu.VMEM((BLOCK + 16, total), f32)],
        compiler_params=params,
        name="conv_back",
    )(dca, dca, halo_back, u, meta, taps)

    grads_late = outer_sum(normed, dall)
    grad_step = jnp.swapaxes(
        grads_late[:, total : total + 2 * heads].reshape(model_width, 2, heads), 1, 2
    ).reshape(model_width, 2 * heads)
    late = [grads_late[:, :inner], grads_late[:, inner:total], grad_step]
    late = jnp.concatenate(
        [v.reshape(model_width, parts, v.shape[1] // parts) for v in late], 2
    ).reshape(model_width, -1)
    late_own = reduce_rows(late, 1)
    grad_proj_value = late_own[:, :own_chan]
    own_state = state_all // parts
    grad_proj_state = gather(late_own[:, own_chan : own_chan + own_state].astype(bf16), 1).astype(f32)
    grad_proj_step = late_own[:, own_chan + own_state :]

    wrest = jnp.concatenate([wv, proj_state, wst], 1)
    tail_in = (res, og, ggate, dall, ng, wg, wrest)
    grad_residual, dng = pl.pallas_call(
        tail_kernel,
        grid=(blocks,),
        in_specs=[
            row_spec(BLOCK, model_width),
            row_spec(BLOCK, model_width),
            row_spec(BLOCK, inner),
            row_spec(BLOCK, wide_total),
        ]
        + [whole_spec(v) for v in tail_in[4:]],
        out_specs=[row_spec(BLOCK, model_width), pl.BlockSpec((8, model_width), lambda c: (0, 0))],
        out_shape=[shaped((length, model_width), f32), shaped((8, model_width), f32)],
        compiler_params=params,
        name="tail",
    )(*tail_in)

    small_grads = [
        dng[0],
        dtaps[:4, inner:].reshape(-1),
        dbias[0, inner:],
        dtaps[:4, :inner].reshape(-1),
        dbias[0, :inner],
        dmix[0],
        dskip_w[:, :heads].reshape(-1),
        dhead[0, : 2 * heads].reshape(2, heads).T.reshape(-1),
        dhead[1, :heads] + dhead[1, heads : 2 * heads],
        dskip_g[0, :heads],
    ]
    flat = lax.psum(jnp.concatenate(small_grads), ("dp", "mp"))
    at, sums = 0, []
    for v in small_grads:
        sums.append(flat[at : at + v.shape[0]])
        at += v.shape[0]

    def own(values, axis):
        size = values.shape[axis] // parts
        return lax.dynamic_slice_in_dim(values, me * size, size, axis)

    return (
        out[:, None, :],
        grad_residual[:, None, :],
        sums[0],
        grad_proj_gate,
        grad_proj_value,
        grad_proj_state,
        grad_proj_step,
        own(sums[3].reshape(4, inner), 1),
        own(sums[4], 0),
        sums[1].reshape(4, state_all),
        sums[2],
        own(sums[7], 0),
        own(sums[8], 0),
        own(sums[9], 0),
        own(sums[6].reshape(inner, heads), 0),
        own(sums[5], 0),
        grad_proj_out,
    )


def solution(mesh):
    return jax.shard_map(
        shards,
        mesh=mesh,
        in_specs=(
            P("mp", "dp", None),
            P("mp", "dp", None),
            P("dp", None),
            P(),
            P(None, "mp"),
            P(None, "mp"),
            P(),
            P(None, "mp"),
            P(None, "mp"),
            P("mp"),
            P(),
            P(),
            P("mp"),
            P("mp"),
            P("mp"),
            P("mp", None),
            P("mp"),
            P("mp", None),
        ),
        out_specs=(
            P("mp", "dp", None),
            P("mp", "dp", None),
            P(),
            P(None, "mp"),
            P(None, "mp"),
            P(),
            P(None, "mp"),
            P(None, "mp"),
            P("mp"),
            P(),
            P(),
            P("mp"),
            P("mp"),
            P("mp"),
            P("mp", None),
            P("mp"),
            P("mp", None),
        ),
        check_vma=False,
    )
```

time: 2490 us -> 708 us (0.28)
  matrix products: 922 us -> 27.8 us
  other arithmetic: 714 us -> 22.6 us
  local copies, waits for them, and re-layouts: 368 us -> 58.5 us
  Pallas kernels: 0 us -> 277 us
  waiting for transfers between devices: 378 us -> 258 us
  blocking collectives: 67.4 us -> 30.8 us
    dot_general x48 -> x3, matrix products: 890 us -> 27.8 us  [outer_sum(): lax.dot_general(left_op, right_op, (((0,), (0,)), ((), ())), preferred_el...]
    another operation x13 -> x2, other arithmetic: 333 us -> 2.35 us  [the longest x8 233 us: segment_sums(): running = jnp.cumsum(jnp.where(lower_mask, repeated, 0.0), axis=-2)]
    pallas_call x0 -> x5, Pallas kernels: none -> 277 us  [the longest x1 87.5 us: shards(): pl.pallas_call(functools.partial(middle_kernel, heads, width, blocks), gr...]
    rev x12 -> x0, local copies, waits for them, and re-layouts: 152 us -> none  [the longest x2 45.6 us: quasiseparable(): return forward_part + backward_part[::-1]]
    reduce_scatter x2 -> x3, waiting for transfers between devices: 145 us -> 0.06 us  [reduce_rows(): lax.psum_scatter(values.astype(bf16), 'mp', scatter_dimension=axis, tiled...]
    reduce_sum x15 -> x1, other arithmetic: 122 us -> 0.31 us  [segment_at(): found = jnp.sum((places[:, None] >= bounds[None, :]).astype(jnp.int32), -1)]
    unnamed x391 -> x66, local copies, waits for them, and re-layouts: 120 us -> 18.1 us
    mul x14 -> x0, other arithmetic: 72.9 us -> none  [the longest x6 47.4 us: short_conv(): kernel[shift_by] * delayed * (delayed_seg == segment)[:, None]]
  transfers between devices with their start and end apart: 8 -> 14, of which waited for: 6 -> 6; matrix products, arithmetic and copies ran while one was open for 30% -> 12% of each run, Pallas kernels for 0% -> 27%
where the time goes in v1:
time: 708 us; the launch traced here: 707 us
  Pallas kernels  277 us (39%)
  waiting for transfers between devices  258 us (36%)
  local copies, waits for them, and re-layouts  58.5 us (8%)
  blocking collectives  30.8 us (4%)
  matrix products  27.8 us (4%)
  other arithmetic  22.6 us (3%)
  starting transfers between devices  16.7 us (2%)
  between operations  15.6 us (2%)
    psum x1, waiting for transfers between devices, shards(): flat = lax.psum(jnp.concatenate(small_grads), ('dp', 'mp'))  118 us
    psum x1, waiting for transfers between devices, reduce_rows(): return lax.psum(mine, 'dp').astype(f32)  101 us
    pallas_call x1, Pallas kernels, shards(): pl.pallas_call(functools.partial(middle_kernel, heads, width, blocks), gr...  87.5 us
    pallas_call x1, Pallas kernels, shards(): pl.pallas_call(functools.partial(scan_back_kernel, heads, width, blocks),...  83.2 us
    pallas_call x1, Pallas kernels, shards(): pl.pallas_call(functools.partial(front_kernel, heads, width, blocks), gri...  49.5 us
    pallas_call x1, Pallas kernels, shards(): pl.pallas_call(tail_kernel, grid=(blocks,), in_specs=[row_spec(BLOCK, mod...  32.5 us
    dot_general x3, matrix products, outer_sum(): lax.dot_general(left_op, right_op, (((0,), (0,)), ((), ())), preferred_el...  27.8 us
    pallas_call x1, Pallas kernels, shards(): pl.pallas_call(functools.partial(conv_back_kernel, blocks), grid=(blocks,...  24.4 us
  transfers between devices with their start and end apart: 14, of which 6 were waited for; matrix products, arithmetic and copies ran while one was open for 12% of the time, Pallas kernels for 27%

profile of v1, /device:TPU:0, one launch (start us, length us, event | category | flops | bytes accessed | tf_op | source)
XLA Modules:
  0.0 706.7 jit_solution(298348844227754861)
XLA Ops:
  9.6 4.9 collective-permute-start
  16.6 7.3 %all-reduce.6 = f32[9312]{0:T(1024)S(1)} all-reduce(f32[9312]{0:T(1024)S(1)} %dynamic-update-slice), channel_id=2, replica_groups=mesh['dp'=16,'mp'=2] {'mp'}, use_global_device_ids=true, to_apply=%add.6 | all-reduce | flops 9312 | bytes 74496
  29.8 5.8 all_gather.22
  40.0 11.3 %all_gather.26 = bf16[1536,24]{1,0:T(8,128)(2,1)S(1)} all-gather(bf16[768,24]{1,0:T(8,128)(2,1)S(1)} %copy.113), channel_id=1, replica_groups=mesh['dp'=16,'mp'=2] {'mp'}, dimensions={0}, use_global_device_ids=true | all-gather | bytes 110592 | tf_op jit(solution)/shard_map/all_gather | solution.py:516
  54.4 49.5 %front.1 = (bf16[2048,768]{1,0:T(8,128)(2,1)}, bf16[2048,1536]{1,0:T(8,128)(2,1)}, bf16[2048,256]{1,0:T(8,128)(2,1)}, bf16[2048,1792]{1,0:T(8,128)(2,1)}, bf16[2...) custom-call(bf16[2048,768]{1,0:T(8,128)(2,1)} %bitcast.63, ...), custom_call_target="tpu_custom_call" | custom-call | tf_op jit(solution)/shard_map/front/pallas_call | solution.py:589
  106.5 4.7 collective-permute-start.1
  111.9 21.4 %all-gather.9.cloned.1.call-done.wo = bf16[1536,768]{1,0:T(8,128)(2,1)} async-done(((bf16[768,768]{1,0:T(8,128)(2,1)}), bf16[1536,768]{1,0:T(8,128)(2,1)}) %all-gather.9.cloned.1.call-update) | async-done | bytes 2359312 | tf_op jit(solution)/shard_map/all_gather | solution.py:516
  134.1 87.5 %middle.1 = (bf16[2048,768]{1,0:T(8,128)(2,1)}, bf16[2048,1536]{1,0:T(8,128)(2,1)}, bf16[2048,1536]{1,0:T(8,128)(2,1)}, bf16[2048,1536]{1,0:T(8,128)(2,1)}, bf16...) custom-call(bf16[2048,768]{1,0:T(8,128)(2,1)} %bitcast.64, ...), custom_call_target="tpu_custom_call" | custom-call | tf_op jit(solution)/shard_map/middle/pallas_call | solution.py:645
  221.6 9.4 %convolution_convert_fusion.2 = bf16[768,1536]{1,0:T(8,128)(2,1)} fusion(bf16[2048,768]{1,0:T(8,128)(2,1)} %get-tuple-element.45.normed_ref, bf16[2048,1536]{1,0:T(8,128)(2,1)} %get-tuple-element.54.ggate), kind=kOutput, calls=%fused_computation.2 | convolution fusion | flops 4833017856 | bytes 11796480 | tf_op jit(solution)/shard_map/dot_general | solution.py:702
  231.1 9.2 %convolution_convert_fusion.1 = bf16[1536,768]{1,0:T(8,128)(2,1)} fusion(bf16[2048,1536]{1,0:T(8,128)(2,1)} %get-tuple-element.72, bf16[2048,1,768]{2,0,1:T(8,128)(2,1)S(1)} %copy-done), kind=kOutput, calls=%fused_computation.1 | convolution fusion | flops 4833017856 | bytes 11796480 | tf_op jit(solution)/shard_map/dot_general | solution.py:702
  246.6 6.6 collective-permute-done.4.dentry_b
  253.2 4.3 collective-permute-done.3.dentry_f
  258.1 83.2 %scan_back.1 = (bf16[2048,1920]{1,0:T(8,128)(2,1)}, f32[8,1792]{1,0:T(8,128)}, f32[8,128]{1,0:T(8,128)}) custom-call(bf16[2048,1536]{1,0:T(8,128)(2,1)} %get-tuple-element.46.x_ref, bf16[2048,256]{1,0:T(8,128)(2,1)} %get-tuple-element.47.g_ref, f32[2048,256]{1,0:T(8,128)} %get-tuple-element.48.rs_ref, f32[2048,128]{1,0:T(8,128)} %pad.23.meta_ref, ...), custom_call_target="tpu_custom_call" | custom-call | tf_op jit(solution)/shard_map/scan_back/pallas_call | solution.py:716
  343.4 4.8 collective-permute-done.5.halo
  348.8 24.4 %conv_back.1 = (bf16[2048,1920]{1,0:T(8,128)(2,1)}, f32[8,1792]{1,0:T(8,128)}) custom-call(bf16[2048,1920]{1,0:T(8,128)(2,1)} %get-tuple-element.61.dca.nxt, bf16[2048,1920]{1,0:T(8,128)(2,1)} %get-tuple-element.61.dca.nxt, bf16[16,1920]{1,0:T(8,128)(2,1)} %copy-done.10, bf16[2048,1792]{1,0:T(8,128)(2,1)} %get-tuple-element.62.u, f32[2048,128]{1,0:T(8,128)} %pad.23.meta_ref, ...), custom_call_target="tpu_custom_call" | custom-call | tf_op jit(solution)/shard_map/conv_back/pallas_call | solution.py:753
  373.2 9.2 %convolution_convert_fusion = bf16[768,1920]{1,0:T(8,128)(2,1)S(1)} fusion(bf16[2048,768]{1,0:T(8,128)(2,1)S(1)} %copy-done.2, bf16[2048,1920]{1,0:T(8,128)(2,1)} %get-tuple-element.63.dall), kind=kOutput, calls=%fused_computation | convolution fusion | flops 6041272320 | bytes 13959168 | tf_op jit(solution)/shard_map/dot_general | solution.py:702
  386.2 5.4 pad_maximum_fusion
  391.6 6.2 copy.118
  407.6 32.5 %tail.1 = (f32[2048,768]{1,0:T(8,128)}, f32[8,768]{1,0:T(8,128)}) custom-call(bf16[2048,768]{1,0:T(8,128)(2,1)} %bitcast.65, bf16[2048,768]{1,0:T(8,128)(2,1)} %bitcast.67, bf16[2048,1536]{1,0:T(8,128)(2,1)} %get-tuple-element.54.ggate, bf16[2048,1920]{1,0:T(8,128)(2,1)} %get-tuple-element.63.dall, f32[1,768]{1,0:T(1,128)} %broadcast_in_dim.71.ng, ...), custom_call_target="tpu_custom_call" | custom-call | tf_op jit(solution)/shard_map/tail/pallas_call | solution.py:787
  442.4 8.5 %copy.119 = f32[2048,1,768]{2,1,0:T(1,128)} copy(f32[2048,1,768]{2,0,1:T(8,128)} %bitcast.69) | data formatting | bytes 12582912
  450.9 118.0 %all-reduce.11.cloned.1.call-done = f32[48224]{0:T(1024)} async-done(((f32[48224]{0:T(1024)}), f32[48224]{0:T(1024)}) %all-reduce.11.cloned.1.call-update) | async-done | bytes 192912 | tf_op jit(solution)/shard_map/psum | solution.py:815
  581.6 100.6 %all-reduce.13.cloned.1.call-done = (bf16[768,920]{0,1:T(8,128)(2,1)}, bf16[768,768]{1,0:T(8,128)(2,1)}, bf16[768,768]{1,0:T(8,128)(2,1)}) async-done(((bf16[768,920]{0,1:T(8,128)(2,1)}, bf16[768,768]{1,0:T(8,128)(2,1)}, bf16[768,768]{1,0:T(8,128)(2,1)}), (bf16[768,920]{0,1:T(8,128)(2,1)}, bf16[768,768]{1,0:T(8,128)(2,1)}, bf16[768,768]{1,0:T(8,128)(2,1)})) %all-reduce.13.cloned.1.call-update) | async-done | bytes 3772432 | tf_op jit(solution)/shard_map/psum | solution.py:706
  686.0 6.4 all_gather.27
  695.4 2.8 convert_element_type.255
  (201 shorter events, 67.3 us)
Async XLA Ops:
  7.2 8.9 %copy-start.19 = (f32[768]{0:T(1024)S(1)}, f32[768]{0:T(1024)}, u32[]{:S(2)}) copy-start(f32[768]{0:T(1024)} %param.34) | copy-start | bytes 9220
  7.3 16.9 %copy-start.24 = (s32[1,7]{1,0:T(1,128)S(1)}, s32[1,7]{1,0:T(1,128)}, u32[]{:S(2)}) copy-start(s32[1,7]{1,0:T(1,128)} %param.20) | copy-start | bytes 88
  7.3 20.0 %copy-start.20 = (f32[256]{0:T(256)S(1)}, f32[256]{0:T(256)}, u32[]{:S(2)}) copy-start(f32[256]{0:T(256)} %param.29) | copy-start | bytes 3076
  7.3 20.0 %copy-start.16 = (f32[4,256]{1,0:T(4,128)S(1)}, f32[4,256]{1,0:T(4,128)}, u32[]{:S(2)}) copy-start(f32[4,256]{1,0:T(4,128)} %param.28) | copy-start | bytes 12292
  7.3 46.5 %all-gather.5.cloned.1.call-start = ((), (), s32[]{:S(2)}) async-start(), calls=%async_computation.3 | async-start | bytes 3538944 | tf_op jit(solution)/shard_map/all_gather | solution.py:516
  8.0 21.8 %copy-start.11 = (bf16[768,24]{0,1:T(8,128)(2,1)S(1)}, bf16[768,24]{0,1:T(8,128)(2,1)}, u32[]{:S(2)}) copy-start(bf16[768,24]{0,1:T(8,128)(2,1)} %param.25) | copy-start | bytes 110596
  8.0 27.6 %copy-start.17 = (f32[768]{0:T(1024)S(1)}, f32[768]{0:T(1024)}, u32[]{:S(2)}) copy-start(f32[768]{0:T(1024)} %param.21) | copy-start | bytes 9220
  8.1 103.8 %all-gather.7.cloned.1.call-start = ((), (), s32[]{:S(2)}) async-start(), calls=%async_computation.4 | async-start | bytes 3538944 | tf_op jit(solution)/shard_map/all_gather | solution.py:516
  8.8 30.3 %copy-start.12 = (bf16[768,24]{0,1:T(8,128)(2,1)S(1)}, bf16[768,24]{0,1:T(8,128)(2,1)}, u32[]{:S(2)}) copy-start(bf16[768,24]{0,1:T(8,128)(2,1)} %param.33) | copy-start | bytes 110596
  8.8 124.5 %all-gather.9.cloned.1.call-start = ((), (), s32[]{:S(2)}) async-start(), calls=%async_computation.5 | async-start | bytes 3538944 | tf_op jit(solution)/shard_map/all_gather | solution.py:516
  9.6 44.2 %collective-permute-start = (bf16[16,768]{1,0:T(8,128)(2,1)S(1)}, bf16[16,768]{1,0:T(8,128)(2,1)S(1)}, u32[]{:S(2)}, u32[]{:S(2)}) collective-permute-start(bf16[16,768]{1,0:T(8,128)(2,1)S(1)} %slice_bitcast_fusion), channel_id=1, source_target_pairs={{0,1},{2,3},{4,5},{6,7},{8,9},{10,11},{12,13},{14,15},{16,17},{18,... | collective-permute-start | bytes 73736 | tf_op jit(solution)/shard_map/ppermute | solution.py:521
  14.5 427.2 %reduce-scatter.4.cloned.1.call-start = ((), (), s32[]{:S(2)}) async-start(), calls=%async_computation.7 | async-start | bytes 3538944 | tf_op jit(solution)/shard_map/reduce_scatter | solution.py:705
  105.2 28.2 %collective-permute-start.2 = (bf16[64,1536]{1,0:T(8,128)(2,1)S(1)}, bf16[64,1536]{1,0:T(8,128)(2,1)S(1)}, u32[]{:S(2)}, u32[]{:S(2)}) collective-permute-start(bf16[64,1536]{1,0:T(8,128)(2,1)S(1)} %get-tuple-element.176), channel_id=1, source_target_pairs={{1,0},{3,2},{5,4},{7,6},{9,8},{11,10},{13,12},{15,14},{17,16},{19,... | collective-permute-start | bytes 589832 | tf_op jit(solution)/shard_map/ppermute | solution.py:632
  106.5 26.9 %collective-permute-start.1 = (bf16[64,1536]{1,0:T(8,128)(2,1)S(1)}, bf16[64,1536]{1,0:T(8,128)(2,1)S(1)}, u32[]{:S(2)}, u32[]{:S(2)}) collective-permute-start(bf16[64,1536]{1,0:T(8,128)(2,1)S(1)} %get-tuple-element.177), channel_id=1, source_target_pairs={{0,1},{2,3},{4,5},{6,7},{8,9},{10,11},{12,13},{14,15},{16,17},{18,... | collective-permute-start | bytes 589832 | tf_op jit(solution)/shard_map/ppermute | solution.py:632
  221.6 9.5 %copy-start = (bf16[2048,1,768]{2,0,1:T(8,128)(2,1)S(1)}, bf16[2048,1,768]{2,0,1:T(8,128)(2,1)}, u32[]{:S(2)}) copy-start(bf16[2048,1,768]{2,0,1:T(8,128)(2,1)} %param.19) | copy-start | bytes 9437188
  231.0 210.7 %reduce-scatter.8.cloned.1.call-start = ((), (), s32[]{:S(2)}) async-start(), calls=%async_computation.9 | async-start | bytes 3538944 | tf_op jit(solution)/shard_map/reduce_scatter | solution.py:705
  240.3 201.4 %reduce-scatter.6.cloned.1.call-start = ((), (), s32[]{:S(2)}) async-start(), calls=%async_computation.8 | async-start | bytes 4239360 | tf_op jit(solution)/shard_map/reduce_scatter | solution.py:705
  241.6 11.5 %collective-permute-start.4 = (bf16[64,1536]{1,0:T(8,128)(2,1)S(1)}, bf16[64,1536]{1,0:T(8,128)(2,1)S(1)}, u32[]{:S(2)}, u32[]{:S(2)}) collective-permute-start(bf16[64,1536]{1,0:T(8,128)(2,1)S(1)} %get-tuple-element.174), channel_id=1, source_target_pairs={{0,1},{2,3},{4,5},{6,7},{8,9},{10,11},{12,13},{14,15},{16,17},{18,... | collective-permute-start | bytes 589832 | tf_op jit(solution)/shard_map/ppermute | solution.py:632
  244.0 13.5 %collective-permute-start.3 = (bf16[64,1536]{1,0:T(8,128)(2,1)S(1)}, bf16[64,1536]{1,0:T(8,128)(2,1)S(1)}, u32[]{:S(2)}, u32[]{:S(2)}) collective-permute-start(bf16[64,1536]{1,0:T(8,128)(2,1)S(1)} %get-tuple-element.175), channel_id=1, source_target_pairs={{1,0},{3,2},{5,4},{7,6},{9,8},{11,10},{13,12},{15,14},{17,16},{19,... | collective-permute-start | bytes 589832 | tf_op jit(solution)/shard_map/ppermute | solution.py:632
  342.1 6.1 collective-permute-start.5
  348.8 24.4 %copy-start.2 = (bf16[2048,768]{1,0:T(8,128)(2,1)S(1)}, bf16[2048,768]{1,0:T(8,128)(2,1)}, u32[]{:S(2)}) copy-start(bf16[2048,768]{1,0:T(8,128)(2,1)} %get-tuple-element.45.normed_ref) | copy-start | bytes 9437188
  397.8 9.8 %copy-start.14 = (f32[8,1792]{1,0:T(8,128)S(1)}, f32[8,1792]{1,0:T(8,128)}, u32[]{:S(2)}) copy-start(f32[8,1792]{1,0:T(8,128)} %get-tuple-element.66) | copy-start | bytes 172036
  397.8 171.1 %all-reduce.11.cloned.1.call-start = ((), (), s32[]{:S(2)}) async-start(), calls=%async_computation.6 | async-start | bytes 393216 | tf_op jit(solution)/shard_map/psum | solution.py:815
  441.6 240.6 %all-reduce.13.cloned.1.call-start = ((), (), s32[]{:S(2)}) async-start(), calls=%async_computation.10 | async-start | bytes 7544832 | tf_op jit(solution)/shard_map/psum | solution.py:706
  (16 other events, 75.7 us)
Sparse Core Ops, SparseCore 0:
  9.6 43.9 all-gather.4
  55.2 36.2 all-gather.6
  93.0 40.2 all-gather.8
  231.1 39.1 reduce-scatter.3
  273.0 34.7 reduce-scatter.7
  397.9 40.0 reduce-scatter.5
  444.1 124.6 all-reduce.10
  572.8 109.3 all-reduce.12
